TPU v7x, 32 devices: a whole 2x2x4 slice. The times are simulated.
32 devices in a mesh: slab: 2 (over x), freq: 4 (over y, core), energy: 4 (over z).
Axes of the slice: x: 2, y: 2, z: 4, core: 2. Of those that a mesh axis runs over, the one named last changes fastest.
Arguments:
- lesser: bfloat16 [8, 4, 2, 512, 512], P('energy', 'slab'), may hold values from -6 to 6
- retarded: bfloat16 [8, 4, 2, 512, 512], P('energy', 'slab'), may hold values from -0.25 to 0.25
- coupling: bfloat16 [8, 512, 512], P('freq'), may hold values from -0.125 to 0.125
- occupations: float32 [8], P('freq'), may hold values from 0.1 to 3
- offsets: int32 [8], P('freq'), may hold values from 1 to 2
- intersection: float32 [4], P('slab'), may hold values from 0.2 to 0.6
Outputs:
- updated: float32 [8, 4, 2, 512, 512], P('energy', 'slab', None, 'freq')
All inputs are finite; a program needn't handle non-finite values.
Results may differ from a plain program's by a relative error of at most 0.017.
Values may be sent and summed in bfloat16 or wider, within the bound.
A program may use at most 128 MiB of HBM per device.

v0:
```python
import functools
import jax
import jax.numpy as jnp
from jax import lax
from jax.experimental import pallas as pl
from jax.experimental.pallas import tpu as pltpu
from jax.sharding import PartitionSpec as P

OFFMAX = 2
UNROLL = 8
MESH = pl.DeviceIdType.MESH
F32 = jnp.float32
BF16 = jnp.bfloat16


def with_halo(block, sides, width):
    for axis, dim in sides:
        count = lax.axis_size(axis)
        forward = [(i, i + 1) for i in range(count - 1)]
        backward = [(target, source) for source, target in forward]
        low = lax.ppermute(
            lax.slice_in_dim(block, block.shape[dim] - width, None, axis=dim), axis, forward
        )
        high = lax.ppermute(lax.slice_in_dim(block, 0, width, axis=dim), axis, backward)
        block = jnp.concatenate([low, block, high], axis=dim)
    return block


def general(lesser, retarded, coupling, occupations, offsets, intersection):
    freq_count = lax.axis_size("freq")
    row_count = lesser.shape[-1] // freq_count
    row_first = lax.axis_index("freq") * row_count
    padded = with_halo(lesser, (("energy", 0),), OFFMAX)
    energy_count = lesser.shape[0]
    positions = jnp.arange(energy_count, dtype=jnp.int32)[None, :] + OFFMAX
    lower_green = jnp.take(padded, positions - offsets[:, None], axis=0)
    upper_green = jnp.take(padded, positions + offsets[:, None], axis=0)
    scale = occupations[:, None, None, None, None, None]
    mixture = (
        scale * lower_green.astype(F32) + (scale + 1.0) * upper_green.astype(F32)
    ).astype(BF16)
    real_green = retarded[:, :, 0]
    imag_green = retarded[:, :, 1]
    real_rows = lax.dynamic_slice_in_dim(real_green, row_first, row_count, 2)
    imag_rows = lax.dynamic_slice_in_dim(imag_green, row_first, row_count, 2)
    left_product = jnp.einsum(
        "fri,fescij->fescrj", coupling, mixture, preferred_element_type=F32
    ).astype(BF16)
    self_energy = lax.psum_scatter(
        jnp.einsum(
            "fescrj,fkj->resck", left_product, coupling, preferred_element_type=F32
        ).astype(BF16),
        "freq",
        scatter_dimension=0,
        tiled=True,
    )
    beside_all = with_halo(self_energy, (("slab", 2),), 1)
    beside = beside_all[:, :, :-2].astype(F32) + beside_all[:, :, 2:].astype(F32)
    total = self_energy.astype(F32) + intersection[None, None, :, None, None] * beside
    combined = total.astype(BF16)
    real_self = combined[:, :, :, 0]
    imag_self = combined[:, :, :, 1]

    def by_transpose(left_side, right_side):
        return jnp.einsum("resj,eskj->resk", left_side, right_side, preferred_element_type=F32)

    real_part = by_transpose(real_self, real_green) + by_transpose(imag_self, imag_green)
    imag_part = by_transpose(imag_self, real_green) - by_transpose(real_self, imag_green)
    product = jnp.stack([real_part, imag_part], axis=3).astype(BF16)
    y_piece = lax.all_gather(product, "freq", axis=0, tiled=True)
    real_piece = y_piece[:, :, :, 0]
    imag_piece = y_piece[:, :, :, 1]

    def plain_product(left_side, right_side):
        return jnp.einsum("esrm,mesk->esrk", left_side, right_side, preferred_element_type=F32)

    out_real = plain_product(real_rows, real_piece) - plain_product(imag_rows, imag_piece)
    out_imag = plain_product(real_rows, imag_piece) + plain_product(imag_rows, real_piece)
    return jnp.stack([out_real, out_imag], axis=2)


def by_rows(a, b):
    return lax.dot_general(a, b, (((1,), (1,)), ((), ())), preferred_element_type=F32)


def kernel(
    chunks, slabs, energies,
    lesser, retarded, coupling, numbers, shifts, beside_weight, out,
    own, low, high, c_buf, w_buf, r_buf, left_buf, acc, half, near, far, comb, result,
    store_sem, local_sem, send_sem, recv_sem,
):
    nf, size, _ = coupling.shape
    cut = size // chunks
    x, q, z = lax.axis_index("slab"), lax.axis_index("freq"), lax.axis_index("energy")
    y, core = q // 2, q % 2
    partner = {"freq": 2 * y + 1 - core}
    across = {"freq": 2 * (1 - y) + core}
    diagonal = {"freq": 2 * (1 - y) + 1 - core}
    opposite = {"slab": 1 - x}
    has_low, has_high = z > 0, z < energies - 1
    below = {"energy": jnp.maximum(z - 1, 0)}
    above = {"energy": jnp.minimum(z + 1, energies - 1)}
    x_to = x + 2 * core - 1
    has_x = jnp.logical_and(x_to >= 0, x_to < slabs)
    beside = {"slab": jnp.clip(x_to, 0, slabs - 1), "freq": 2 * y + 1 - core}

    barrier = pltpu.get_barrier_semaphore()
    peers = [(None, partner), (None, across), (None, diagonal), (None, opposite), (has_low, below), (has_high, above), (has_x, beside)]

    def under(condition, action):
        if condition is None:
            action()
        else:
            pl.when(condition)(action)

    for condition, peer in peers:
        under(condition, lambda peer=peer: pl.semaphore_signal(barrier, inc=1, device_id=peer, device_id_type=MESH))

    count = [0]

    def remote(src, dst, peer):
        n = count[0]
        count[0] += 1
        return pltpu.make_async_remote_copy(
            src_ref=src, dst_ref=dst, send_sem=send_sem.at[n], recv_sem=recv_sem.at[n],
            device_id=peer, device_id_type=MESH,
        )

    load_own = pltpu.make_async_copy(lesser.at[:, core, y], own, local_sem.at[0])
    load_c = [
        pltpu.make_async_copy(
            coupling.at[i, :, pl.ds(k * cut, cut)],
            c_buf.at[k, :, pl.ds(i * cut, cut)],
            local_sem.at[3 + i * chunks + k],
        )
        for i in range(nf)
        for k in range(chunks)
    ]
    load_r = pltpu.make_async_copy(retarded, r_buf, local_sem.at[1])
    for load in [load_own] + load_c:
        load.start()

    for i in range(nf):
        number, shift = numbers[i], shifts[i]
        none = jnp.float32(0.0)
        row = [
            jnp.where(shift == 1, number, none),
            jnp.where(shift == 2, number, none),
            jnp.where(shift == 1, number + 1.0, none),
            jnp.where(shift == 2, number + 1.0, none),
        ]
        for j in range(8):
            w_buf[i, j : j + 1, :] = jnp.full((1, cut), row[j % 4], F32)

    def zero(ref):
        ref[...] = jnp.zeros_like(ref)

    pl.when(jnp.logical_not(has_low))(lambda: zero(low))
    pl.when(jnp.logical_not(has_high))(lambda: zero(high))

    greeted = 4 + sum(condition.astype(jnp.int32) for condition in (has_low, has_high, has_x))
    pl.semaphore_wait(barrier, greeted)

    sent = []

    def go(copy, condition=None):
        under(condition, copy.start)
        sent.append((condition, copy))
        return copy

    w_in = [
        go(remote(w_buf.at[pl.ds(0, nf)], w_buf.at[pl.ds(slot * nf, nf)], peer))
        for slot, peer in ((1, partner), (2, across), (3, diagonal))
    ]

    def part(slot, k):
        start = slot * cut
        return c_buf.at[k, :, pl.ds(start if isinstance(start, int) else pl.multiple_of(start, cut), cut)]

    ups, downs, c_across, c_near = [], [], [], []
    for k in range(chunks):
        columns = pl.ds(k * cut, cut)
        c_across.append(go(remote(coupling.at[x, :, columns], part(2 * nf + x, k), across)))
    for k in range(chunks):
        columns = pl.ds(k * cut, cut)
        for i in range(nf):
            c_near.append(go(remote(coupling.at[i, :, columns], part(nf + i, k), partner)))
        ups.append(go(remote(lesser.at[:, core, y, :, columns], low.at[k], above), has_high))
        downs.append(go(remote(lesser.at[:, core, y, :, columns], high.at[k], below), has_low))

    load_r.start()
    load_own.wait()
    for load in load_c:
        load.wait()
    for copy in w_in:
        copy.wait_recv()

    def terms(k, e):
        columns = slice(k * cut, (k + 1) * cut)
        if e == 0:
            return low.at[k, 1], low.at[k, 0], own.at[1, :, columns], high.at[k, 0]
        return own.at[0, :, columns], low.at[k, 1], high.at[k, 0], high.at[k, 1]

    def left_side(k, e, number, slot_of):
        refs = terms(k, e)

        def body(j, carry):
            f = slot_of(j)
            w = w_buf[f]
            mixed = w[0:1] * refs[0][...].astype(F32)
            for i in (1, 2, 3):
                mixed = mixed + w[i : i + 1] * refs[i][...].astype(F32)
            columns = pl.ds(pl.multiple_of(f * cut, cut), cut)
            whole = jnp.concatenate([c_buf[h, :, columns] for h in range(chunks)], axis=1)
            left = jnp.dot(whole, mixed.astype(BF16), preferred_element_type=F32)
            left_buf[e, :, columns] = left.astype(BF16)
            return carry

        lax.fori_loop(0, number, body, 0, unroll=min(UNROLL, number))

    def right_side(k, e):
        return by_rows(left_buf[e], c_buf[k])

    def arrive(k):
        pl.when(has_low)(ups[k].wait_recv)
        pl.when(has_high)(downs[k].wait_recv)

    relayed, c_far = [], []
    for k in range(chunks):
        c_across[k].wait_recv()
        relayed.append(go(remote(part(2 * nf + x, k), part(2 * nf + x, k), opposite)))
        c_far.append(go(remote(part(2 * nf + x, k), part(3 * nf + x, k), partner)))
    arrive(0)
    for copy in c_near:
        copy.wait_recv()
    for e in range(2):
        left_side(0, e, 2 * nf, lambda j: j)
    other_x = 1 - x
    c_rest = []
    for k in range(chunks):
        relayed[k].wait_recv()
        c_rest.append(go(remote(part(2 * nf + other_x, k), part(3 * nf + other_x, k), partner)))
    for copy in c_far + c_rest:
        copy.wait_recv()
    for e in range(2):
        left_side(0, e, 2 * nf, lambda j: 2 * nf + j)
        acc[e] = right_side(0, e)

    for k in range(1, chunks - 1):
        arrive(k)
        for e in range(2):
            left_side(k, e, 4 * nf, lambda j: j)
            acc[e] += right_side(k, e)

    pairs = [(e, h) for e in range(2) for h in range(2)]
    to_far = {p: remote(half.at[p], far.at[p], beside) for p in pairs}
    to_near = {p: remote(half.at[p], near.at[p], partner) for p in pairs}
    comb_across = {(e, h): remote(comb.at[e, 0, h], comb.at[e, 2, h], across) for e, h in pairs}
    comb_near = {(e, h): remote(comb.at[e, 0, h], comb.at[e, 1, h], partner) for e, h in pairs}
    comb_far = {(e, h): remote(comb.at[e, 2, h], comb.at[e, 3, h], partner) for e, h in pairs}
    last = chunks - 1
    middle_column = size // 2

    def finish_self(e, h):
        columns = slice(h * middle_column, (h + 1) * middle_column)
        total = acc[e, :, columns] + by_rows(left_buf[e], c_buf[last, columns, :])
        half[e, h] = total.astype(BF16)
        go(to_far[e, h], has_x)
        go(to_near[e, h])

    def combine(e, h, with_far):
        to_near[e, h].wait_recv()
        around = near[e, h].astype(F32)
        if with_far:
            to_far[e, h].wait_recv()
            around = around + far[e, h].astype(F32)
        comb[e, 0, h] = (half[e, h].astype(F32) + beside_weight[core] * around).astype(BF16)
        comb_across[e, h].start()
        comb_near[e, h].start()

    alone = jnp.logical_not(has_x)

    def combine_alone(e, h):
        pl.when(alone)(lambda: combine(e, h, False))

    arrive(last)
    left_side(last, 0, 4 * nf, lambda j: j)
    finish_self(0, 0)
    finish_self(0, 1)
    combine_alone(0, 0)
    left_side(last, 1, 4 * nf, lambda j: j)
    combine_alone(0, 1)
    finish_self(1, 0)
    finish_self(1, 1)
    combine_alone(1, 0)
    combine_alone(1, 1)
    for e, h in pairs:
        pl.when(has_x)(lambda e=e, h=h: combine(e, h, True))

    load_r.wait()
    rows = size // 4
    mine = pl.ds(pl.multiple_of(q * rows, rows), rows)

    def pass_on(e):
        for h in range(2):
            comb_across[e, h].wait_recv()
            comb_far[e, h].start()

    def take(e):
        for h in range(2):
            comb_near[e, h].wait_recv()
            comb_far[e, h].wait_recv()

    def whole_sum(e, slot):
        return jnp.concatenate([comb[e, slot, 0], comb[e, slot, 1]], axis=1)

    stores = []

    for group in range(2):
        same = alone if group == 0 else has_x
        s = x if group == 0 else 1 - x
        other = jnp.where(same, 0, 1)
        for e in range(2):
            pl.when(same)(lambda e=e: pass_on(e))
            pl.when(jnp.logical_not(same))(lambda e=e: take(e))
            edge = jnp.concatenate([r_buf[e, s, 0, mine, :], r_buf[e, s, 1, mine, :]], axis=0)
            with_real = jnp.dot(edge, whole_sum(e, 2 * y + other), preferred_element_type=F32)
            with_imag = jnp.dot(edge, whole_sum(e, 2 * (1 - y) + other), preferred_element_type=F32)
            middle = jnp.concatenate(
                [with_real[:rows] - with_imag[rows:], with_imag[:rows] + with_real[rows:]], axis=0
            ).astype(BF16)
            by_real = by_rows(middle, r_buf[e, s, 0])
            by_imag = by_rows(middle, r_buf[e, s, 1])
            result[e, group, 0] = (by_real[:rows] + by_imag[rows:]).astype(BF16)
            result[e, group, 1] = (by_real[rows:] - by_imag[:rows]).astype(BF16)
            store = pltpu.make_async_copy(result.at[e, group], out.at[e, s], store_sem.at[e, group])
            store.start()
            stores.append(store)

    for copies in (comb_across, comb_near, comb_far):
        for p in pairs:
            copies[p].wait_send()
    for store in stores:
        store.wait()
    for condition, copy in sent:
        under(condition, copy.wait_send)


def fast(lesser, retarded, coupling, occupations, offsets, intersection):
    nf, size, _ = coupling.shape
    chunks = 2
    cut = size // chunks
    copies = 3 + (nf + 6) * chunks + 20
    anywhere = pl.BlockSpec(memory_space=pl.ANY)
    return pl.pallas_call(
        functools.partial(kernel, chunks, lax.axis_size("slab"), lax.axis_size("energy")),
        out_shape=jax.ShapeDtypeStruct((2, 2, 2, size // 4, size), BF16),
        in_specs=[anywhere] * 3 + [pl.BlockSpec(memory_space=pltpu.SMEM)] * 3,
        out_specs=anywhere,
        scratch_shapes=[
            pltpu.VMEM((2, size, size), BF16),
            pltpu.VMEM((chunks, 2, size, cut), BF16),
            pltpu.VMEM((chunks, 2, size, cut), BF16),
            pltpu.VMEM((chunks, size, 4 * nf * cut), BF16),
            pltpu.VMEM((4 * nf, 8, cut), F32),
            pltpu.VMEM((2, 2, 2, size, size), BF16),
            pltpu.VMEM((2, size, 4 * nf * cut), BF16),
            pltpu.VMEM((2, size, size), F32),
            pltpu.VMEM((2, 2, size, size // 2), BF16),
            pltpu.VMEM((2, 2, size, size // 2), BF16),
            pltpu.VMEM((2, 2, size, size // 2), BF16),
            pltpu.VMEM((2, 4, 2, size, size // 2), BF16),
            pltpu.VMEM((2, 2, 2, size // 4, size), BF16),
            pltpu.SemaphoreType.DMA((2, 2)),
            pltpu.SemaphoreType.DMA((3 + nf * chunks,)),
            pltpu.SemaphoreType.DMA((copies,)),
            pltpu.SemaphoreType.DMA((copies,)),
        ],
        compiler_params=pltpu.CompilerParams(
            collective_id=0, has_side_effects=True, vmem_limit_bytes=60 << 20
        ),
    )(lesser, retarded, coupling, occupations, offsets, intersection).astype(F32)


def solution(mesh):
    def shards(lesser, retarded, *rest):
        fits = (
            (mesh.shape["slab"], mesh.shape["freq"]) == (2, 4)
            and lesser.shape[:2] == (2, 2)
            and lesser.shape[-1] == 512
            and rest[0].shape[0] == 2
        )
        return (fast if fits else general)(lesser, retarded, *rest)

    return jax.shard_map(
        shards,
        mesh=mesh,
        in_specs=(
            P("energy", "slab", None, None, None),
            P("energy", "slab", None, None, None),
            P("freq", None, None),
            P("freq"),
            P("freq"),
            P("slab"),
        ),
        out_specs=P("energy", "slab", None, "freq", None),
        check_vma=False,
    )
```

profile of v0, /device:TPU:0, one launch (start us, length us, event | category | flops | bytes accessed | tf_op | source)
XLA Modules:
  0.0 65.3 jit_solution(17065191589711349963)
XLA Ops:
  0.0 62.5 %shard_map.64 = bf16[2,2,2,128,512]{4,3,2,1,0:T(8,128)(2,1)} custom-call(bf16[2,2,2,512,512]{4,3,2,1,0:T(8,128)(2,1)} %lesser.1, bf16[2,2,2,512,512]{4,3,2,1,0:T(8,128)(2,1)} %retarded.1, bf16[2,512,512]{2,1,0:T(8,128)(2,1)} %coupling.1, f32[2]{0:T(128)} %numbers.1, s32[2]{0:T(128)} %shifts.1, f32[2]{0:T(128)} %beside_weight.1), custom_call_target="tpu_custom_call" | custom-call | tf_op jit(solution)/shard_map/pallas_call | solution.py:355
  62.5 2.8 %convert_element_type.3 = f32[2,2,2,128,512]{4,3,2,1,0:T(8,128)} convert(bf16[2,2,2,128,512]{4,3,2,1,0:T(8,128)(2,1)} %shard_map.64) | non-fusion elementwise | flops 524288 | bytes 3145728 | tf_op jit(solution)/shard_map/convert_element_type | solution.py:382
where the time goes:
time: 65.5 us; the launch traced here: 65.3 us
  Pallas kernels  62.5 us (95%)
  other arithmetic  2.83 us (4%)
    pallas_call x1, Pallas kernels, fast(): pl.pallas_call(functools.partial(kernel, chunks, lax.axis_size('slab'), l...  62.5 us
    convert_element_type x1, other arithmetic, fast(): return pl.pallas_call(functools.partial(kernel, chunks, lax.axis_size('sl...  2.83 us

commit v1 on v0

v1 whole, which is shorter than its diff:
```python
import functools
import jax
import jax.numpy as jnp
from jax import lax
from jax.experimental import pallas as pl
from jax.experimental.pallas import tpu as pltpu
from jax.sharding import PartitionSpec as P

OFFMAX = 2
UNROLL = 8
PIECES = 3
BLOCKS = 4
MESH = pl.DeviceIdType.MESH
F32 = jnp.float32
BF16 = jnp.bfloat16


def with_halo(block, sides, width):
    for axis, dim in sides:
        count = lax.axis_size(axis)
        forward = [(i, i + 1) for i in range(count - 1)]
        backward = [(target, source) for source, target in forward]
        low = lax.ppermute(
            lax.slice_in_dim(block, block.shape[dim] - width, None, axis=dim), axis, forward
        )
        high = lax.ppermute(lax.slice_in_dim(block, 0, width, axis=dim), axis, backward)
        block = jnp.concatenate([low, block, high], axis=dim)
    return block


def general(lesser, retarded, coupling, occupations, offsets, intersection):
    freq_count = lax.axis_size("freq")
    row_count = lesser.shape[-1] // freq_count
    row_first = lax.axis_index("freq") * row_count
    padded = with_halo(lesser, (("energy", 0),), OFFMAX)
    energy_count = lesser.shape[0]
    positions = jnp.arange(energy_count, dtype=jnp.int32)[None, :] + OFFMAX
    lower_green = jnp.take(padded, positions - offsets[:, None], axis=0)
    upper_green = jnp.take(padded, positions + offsets[:, None], axis=0)
    scale = occupations[:, None, None, None, None, None]
    mixture = (
        scale * lower_green.astype(F32) + (scale + 1.0) * upper_green.astype(F32)
    ).astype(BF16)
    real_green = retarded[:, :, 0]
    imag_green = retarded[:, :, 1]
    real_rows = lax.dynamic_slice_in_dim(real_green, row_first, row_count, 2)
    imag_rows = lax.dynamic_slice_in_dim(imag_green, row_first, row_count, 2)
    left_product = jnp.einsum(
        "fri,fescij->fescrj", coupling, mixture, preferred_element_type=F32
    ).astype(BF16)
    self_energy = lax.psum_scatter(
        jnp.einsum(
            "fescrj,fkj->resck", left_product, coupling, preferred_element_type=F32
        ).astype(BF16),
        "freq",
        scatter_dimension=0,
        tiled=True,
    )
    beside_all = with_halo(self_energy, (("slab", 2),), 1)
    beside = beside_all[:, :, :-2].astype(F32) + beside_all[:, :, 2:].astype(F32)
    total = self_energy.astype(F32) + intersection[None, None, :, None, None] * beside
    combined = total.astype(BF16)
    real_self = combined[:, :, :, 0]
    imag_self = combined[:, :, :, 1]

    def by_transpose(left_side, right_side):
        return jnp.einsum("resj,eskj->resk", left_side, right_side, preferred_element_type=F32)

    real_part = by_transpose(real_self, real_green) + by_transpose(imag_self, imag_green)
    imag_part = by_transpose(imag_self, real_green) - by_transpose(real_self, imag_green)
    product = jnp.stack([real_part, imag_part], axis=3).astype(BF16)
    y_piece = lax.all_gather(product, "freq", axis=0, tiled=True)
    real_piece = y_piece[:, :, :, 0]
    imag_piece = y_piece[:, :, :, 1]

    def plain_product(left_side, right_side):
        return jnp.einsum("esrm,mesk->esrk", left_side, right_side, preferred_element_type=F32)

    out_real = plain_product(real_rows, real_piece) - plain_product(imag_rows, imag_piece)
    out_imag = plain_product(real_rows, imag_piece) + plain_product(imag_rows, real_piece)
    return jnp.stack([out_real, out_imag], axis=2)


def by_rows(a, b):
    return lax.dot_general(a, b, (((1,), (1,)), ((), ())), preferred_element_type=F32)


def kernel(
    chunks, energies,
    lesser, retarded, coupling, numbers, shifts, beside_weight, out,
    green, c_buf, w_buf, r_buf, left_buf, acc, edge_own, edge_other, near_own, near_other,
    comb, rows_of, middle, result,
    store_sem, local_sem, send_sem, recv_sem,
):
    nf, size, _ = coupling.shape
    cut = size // chunks
    half = size // 2
    x, q, z = lax.axis_index("slab"), lax.axis_index("freq"), lax.axis_index("energy")
    y, core = q // 2, q % 2
    outer, edge = x, 1 - x
    partner = {"freq": 2 * y + 1 - core}
    across = {"freq": 2 * (1 - y) + core}
    diagonal = {"freq": 2 * (1 - y) + 1 - core}
    opposite = {"slab": 1 - x}
    has_low, has_high = z > 0, z < energies - 1
    below = {"energy": jnp.maximum(z - 1, 0)}
    above = {"energy": jnp.minimum(z + 1, energies - 1)}
    first = core == 0
    second = core == 1
    has_to = jnp.logical_or(jnp.logical_and(first, has_high), jnp.logical_and(second, has_low))
    has_from = jnp.logical_or(jnp.logical_and(first, has_low), jnp.logical_and(second, has_high))
    along = {"energy": jnp.clip(z + 1 - 2 * core, 0, energies - 1)}

    barrier = pltpu.get_barrier_semaphore()
    peers = [(None, partner), (None, across), (None, diagonal), (None, opposite), (has_low, below), (has_high, above)]

    def under(condition, action):
        if condition is None:
            action()
        else:
            pl.when(condition)(action)

    for condition, peer in peers:
        under(condition, lambda peer=peer: pl.semaphore_signal(barrier, inc=1, device_id=peer, device_id_type=MESH))

    count = [0, 0]

    def remote(src, dst, peer):
        n = count[0]
        count[0] += 1
        return pltpu.make_async_remote_copy(
            src_ref=src, dst_ref=dst, send_sem=send_sem.at[n], recv_sem=recv_sem.at[n],
            device_id=peer, device_id_type=MESH,
        )

    def local(src, dst):
        n = count[1]
        count[1] += 1
        return pltpu.make_async_copy(src, dst, local_sem.at[n])

    def part(slot, k):
        return c_buf.at[k, :, pl.ds(slot * cut, cut)]

    pieces = [(edge, y), (outer, y), (outer, 1 - y)]
    near_slot, far_slot, own_slot = 2 * core, 2 * core + 1, 2 - 2 * core
    passed_slot, pass_to = 3 - 2 * core, 1 + 2 * core
    columns_of = [pl.ds(k * cut, cut) for k in range(chunks)]
    load_own = [
        [local(lesser.at[1 - core, s, c, :, columns_of[k]], green.at[p, k, own_slot]) for k in range(chunks)]
        for p, (s, c) in enumerate(pieces)
    ]
    load_c = [local(coupling.at[i, :, columns_of[k]], part(i, k)) for i in range(nf) for k in range(chunks)]
    load_r = [
        local(retarded.at[e, s, c], r_buf.at[e, s, :, pl.ds(c * size, size)])
        for e in range(2)
        for s in range(2)
        for c in range(2)
    ]
    for load in load_c + load_own[0]:
        load.start()

    for i in range(nf):
        number, shift = numbers[i], shifts[i]
        none = jnp.float32(0.0)
        row = [
            jnp.where(shift == 1, number, none),
            jnp.where(shift == 2, number, none),
            jnp.where(shift == 1, number + 1.0, none),
            jnp.where(shift == 2, number + 1.0, none),
        ]
        for j in range(8):
            w_buf[i, j : j + 1, :] = jnp.full((1, cut), row[j % 4], F32)

    def zero(p, k, slot):
        green[p, k, slot] = jnp.zeros((size, cut), BF16)

    for p in range(PIECES):
        for k in range(chunks):
            pl.when(jnp.logical_not(has_from))(lambda p=p, k=k: zero(p, k, near_slot))
            pl.when(jnp.logical_not(has_from))(lambda p=p, k=k: zero(p, k, far_slot))
            pl.when(jnp.logical_not(has_to))(lambda p=p, k=k: zero(p, k, passed_slot))

    greeted = 4 + sum(condition.astype(jnp.int32) for condition in (has_low, has_high))
    pl.semaphore_wait(barrier, greeted)

    sent = []

    def go(copy, condition=None):
        under(condition, copy.start)
        sent.append((condition, copy))
        return copy

    depth = size // BLOCKS
    blocks = [(k, pl.ds(r * depth, depth)) for k in range(chunks) for r in range(BLOCKS)]

    def block(slot, b):
        k, rows = blocks[b]
        return c_buf.at[k, rows, pl.ds(slot * cut, cut)]

    c_across = [go(remote(coupling.at[x, rows, columns_of[k]], block(4, b), across)) for b, (k, rows) in enumerate(blocks)]
    near, far, passed = {}, {}, {}
    for p, (s, c) in enumerate(pieces):
        for k in range(chunks):
            near[p, k] = go(remote(lesser.at[1 - core, s, c, :, columns_of[k]], green.at[p, k, near_slot], along), has_to)
            far[p, k] = go(remote(lesser.at[core, s, c, :, columns_of[k]], green.at[p, k, far_slot], along), has_to)
            passed[p, k] = remote(green.at[p, k, near_slot], green.at[p, k, pass_to], partner)
    w_in = [go(remote(w_buf.at[pl.ds(0, nf)], w_buf.at[pl.ds(nf, nf)], partner))]
    for i in range(nf):
        slot = 4 + 2 * (x if i == 0 else 1 - x)
        w_in.append(go(remote(w_buf.at[i], w_buf.at[slot], across)))
        w_in.append(go(remote(w_buf.at[i], w_buf.at[slot + 1], diagonal)))
    c_near = [go(remote(coupling.at[i, :, columns_of[k]], part(nf + i, k), partner)) for i in range(nf) for k in range(chunks)]
    for load in load_own[1] + load_own[2] + load_r:
        load.start()

    relayed = [remote(block(4, b), block(6, b), opposite) for b in range(len(blocks))]
    c_far = [remote(part(4, k), part(5, k), partner) for k in range(chunks)]
    c_rest = [remote(part(6, k), part(7, k), partner) for k in range(chunks)]

    def pump(b):
        c_across[b].wait_recv()
        go(relayed[b])
        if b % BLOCKS == BLOCKS - 1:
            go(c_far[b // BLOCKS])

    def rest(k):
        for b in range(k * BLOCKS, (k + 1) * BLOCKS):
            relayed[b].wait_recv()
        go(c_rest[k])

    def pass_on(p, k):
        pl.when(has_from)(near[p, k].wait_recv)
        go(passed[p, k], has_from)

    def arrive(p, k):
        pl.when(has_from)(far[p, k].wait_recv)
        pl.when(has_to)(passed[p, k].wait_recv)

    def left_side(p, k, start, stop):
        def body(f, carry):
            w = w_buf[f]
            mixed = w[0:1] * green[p, k, 0].astype(F32)
            for i in (1, 2, 3):
                mixed = mixed + w[i : i + 1] * green[p, k, i].astype(F32)
            columns = pl.ds(pl.multiple_of(f * cut, cut), cut)
            whole = jnp.concatenate([c_buf[h, :, columns] for h in range(chunks)], axis=1)
            left = jnp.dot(whole, mixed.astype(BF16), preferred_element_type=F32)
            left_buf[k, :, columns] = left.astype(BF16)
            return carry

        lax.fori_loop(start, stop, body, 0, unroll=min(UNROLL, stop - start))

    def right_side(k, start, stop, rows=slice(None)):
        columns = slice(start * cut, stop * cut)
        return by_rows(left_buf[k, :, columns], c_buf[k, rows, columns])

    halves = [slice(h * half, (h + 1) * half) for h in range(2)]
    to_across = [remote(edge_own.at[h], edge_other.at[h], across) for h in range(2)]
    to_beside = [remote(edge_own.at[h], near_own.at[h], opposite) for h in range(2)]
    over_across = remote(near_own.at[1], near_other.at[1], across)
    over_beside = remote(edge_other.at[0], near_other.at[0], opposite)
    to_partner = {
        (s, c, h): remote(comb.at[0, s, c, h], comb.at[1, s, c, h], partner)
        for s in range(2)
        for c in range(2)
        for h in range(2)
    }
    weight_outer, weight_edge = beside_weight[outer], beside_weight[edge]
    last = chunks - 1

    pump(0)
    pump(1)
    pass_on(0, 0)
    pump(2)
    pump(3)
    for load in load_c + load_own[0]:
        load.wait()
    for copy in w_in + c_near:
        copy.wait_recv()
    arrive(0, 0)
    left_side(0, 0, 0, 2)
    pump(4)
    left_side(0, 0, 2, 4)
    pump(5)
    acc[0] = right_side(0, 0, 4)
    pass_on(0, 1)
    rest(0)
    pump(6)
    pump(7)
    arrive(0, 1)
    left_side(0, 1, 0, 4)
    acc[0] += right_side(1, 0, 4)
    for copy in c_far:
        copy.wait_recv()
    left_side(0, 0, 4, 6)
    left_side(0, 1, 4, 6)
    acc[0] += right_side(0, 4, 6) + right_side(1, 4, 6)
    rest(1)
    pass_on(1, 0)
    for copy in c_rest:
        copy.wait_recv()
    left_side(0, 0, 6, 8)
    left_side(0, 1, 6, 8)
    for h in range(2):
        total = acc[0, :, halves[h]] + (right_side(0, 6, 8, halves[h]) + right_side(1, 6, 8, halves[h]))
        edge_own[h] = total.astype(BF16)
        go(to_across[h])
        if h == 1:
            go(to_beside[1])
            go(to_beside[0])

    for load in load_own[1] + load_own[2] + load_r:
        load.wait()
    rows = size // 4
    mine = pl.ds(pl.multiple_of(q * rows, rows), rows)
    here = y == 0
    for n, e in enumerate((core, 1 - core)):
        for m, s in enumerate((outer, edge)):
            real, imag = r_buf[e, s, mine, :size], r_buf[e, s, mine, size:]
            rows_of[n, m, 0] = jnp.concatenate([jnp.where(here, real, -imag), jnp.where(here, imag, real)], axis=0)
            rows_of[n, m, 1] = jnp.concatenate([jnp.where(here, -imag, real), jnp.where(here, real, imag)], axis=0)

    arrive(1, 0)
    left_side(1, 0, 0, 8)
    acc[1] = right_side(0, 0, 8)
    pass_on(1, 1)
    arrive(1, 1)
    left_side(1, 1, 0, 8)
    for h in range(2):
        total = acc[1, :, halves[h]] + right_side(last, 0, 8, halves[h])
        own = edge_own[h].astype(F32)
        comb[0, 0, 0, h] = (total + weight_outer * own).astype(BF16)
        go(to_partner[0, 0, h])
        acc[1, :, halves[h]] = own + weight_edge * total
    to_beside[1].wait_recv()
    go(over_across)
    to_across[0].wait_recv()
    go(over_beside)
    pass_on(2, 0)
    arrive(2, 0)
    left_side(2, 0, 0, 8)
    acc[0] = right_side(0, 0, 8)

    def project(n, m, c, h):
        return jnp.dot(rows_of[n, m, c], comb[n, m, c, h], preferred_element_type=F32)

    to_beside[0].wait_recv()
    for h in range(2):
        comb[0, 1, 0, h] = (acc[1, :, halves[h]] + weight_edge * near_own[h].astype(F32)).astype(BF16)
        go(to_partner[1, 0, h])
    pass_on(2, 1)
    for n in range(2):
        for m in range(2):
            for h in range(2):
                if n == 1:
                    to_partner[m, 0, h].wait_recv()
                middle[n, m, :, halves[h]] = project(n, m, 0, h)
    to_across[1].wait_recv()
    arrive(2, 1)
    left_side(2, 1, 0, 8)
    over_across.wait_recv()
    over_beside.wait_recv()
    for h in range(2):
        total = acc[0, :, halves[h]] + right_side(last, 0, 8, halves[h])
        other = edge_other[h].astype(F32)
        comb[0, 0, 1, h] = (total + weight_outer * other).astype(BF16)
        go(to_partner[0, 1, h])
        comb[0, 1, 1, h] = (other + weight_edge * (total + near_other[h].astype(F32))).astype(BF16)
        go(to_partner[1, 1, h])

    stores = []
    for n, e in enumerate((core, 1 - core)):
        for m, s in enumerate((outer, edge)):
            whole = []
            for h in range(2):
                if n == 1:
                    to_partner[m, 1, h].wait_recv()
                whole.append((middle[n, m, :, halves[h]] + project(n, m, 1, h)).astype(BF16))
            both = jnp.concatenate(whole, axis=1)
            real, imag = both[:rows], both[rows:]
            sides = jnp.concatenate(
                [jnp.concatenate([real, imag], axis=1), jnp.concatenate([imag, -real], axis=1)], axis=0
            )
            updated = by_rows(sides, r_buf[e, s]).astype(BF16)
            result[n, m, 0] = updated[:rows]
            result[n, m, 1] = updated[rows:]
            store = pltpu.make_async_copy(result.at[n, m], out.at[e, s], store_sem.at[n, m])
            store.start()
            stores.append(store)

    for store in stores:
        store.wait()
    for condition, copy in sent:
        under(condition, copy.wait_send)


def fast(lesser, retarded, coupling, occupations, offsets, intersection):
    nf, size, _ = coupling.shape
    chunks = 2
    cut = size // chunks
    rows = size // 4
    copies = chunks * (2 * BLOCKS + 3 * PIECES + 2 + nf) + 1 + 2 * nf + 14
    loads = PIECES * chunks + nf * chunks + 8
    anywhere = pl.BlockSpec(memory_space=pl.ANY)
    return pl.pallas_call(
        functools.partial(kernel, chunks, lax.axis_size("energy")),
        out_shape=jax.ShapeDtypeStruct((2, 2, 2, rows, size), BF16),
        in_specs=[anywhere] * 3 + [pl.BlockSpec(memory_space=pltpu.SMEM)] * 3,
        out_specs=anywhere,
        scratch_shapes=[
            pltpu.VMEM((PIECES, chunks, 4, size, cut), BF16),
            pltpu.VMEM((chunks, size, 4 * nf * cut), BF16),
            pltpu.VMEM((4 * nf, 8, cut), F32),
            pltpu.VMEM((2, 2, size, 2 * size), BF16),
            pltpu.VMEM((chunks, size, 4 * nf * cut), BF16),
            pltpu.VMEM((2, size, size), F32),
            pltpu.VMEM((2, size, size // 2), BF16),
            pltpu.VMEM((2, size, size // 2), BF16),
            pltpu.VMEM((2, size, size // 2), BF16),
            pltpu.VMEM((2, size, size // 2), BF16),
            pltpu.VMEM((2, 2, 2, 2, size, size // 2), BF16),
            pltpu.VMEM((2, 2, 2, 2 * rows, size), BF16),
            pltpu.VMEM((2, 2, 2 * rows, size), F32),
            pltpu.VMEM((2, 2, 2, rows, size), BF16),
            pltpu.SemaphoreType.DMA((2, 2)),
            pltpu.SemaphoreType.DMA((loads,)),
            pltpu.SemaphoreType.DMA((copies,)),
            pltpu.SemaphoreType.DMA((copies,)),
        ],
        compiler_params=pltpu.CompilerParams(
            collective_id=0, has_side_effects=True, vmem_limit_bytes=60 << 20
        ),
    )(lesser, retarded, coupling, occupations, offsets, intersection).astype(F32)


def solution(mesh):
    def shards(lesser, retarded, *rest):
        fits = (
            (mesh.shape["slab"], mesh.shape["freq"]) == (2, 4)
            and lesser.shape[:2] == (2, 2)
            and lesser.shape[-1] == 512
            and rest[0].shape[0] == 2
        )
        return (fast if fits else general)(lesser, retarded, *rest)

    return jax.shard_map(
        shards,
        mesh=mesh,
        in_specs=(
            P("energy", "slab", None, None, None),
            P("energy", "slab", None, None, None),
            P("freq", None, None),
            P("freq"),
            P("freq"),
            P("slab"),
        ),
        out_specs=P("energy", "slab", None, "freq", None),
        check_vma=False,
    )
```

time: 65.5 us -> 58.9 us (0.90)
  Pallas kernels: 62.5 us -> 55.9 us
    pallas_call x1, Pallas kernels: 62.5 us -> 55.9 us  [fast(): pl.pallas_call(functools.partial(kernel, chunks, lax.axis_size('energy'))...]
where the time goes in v1:
time: 58.9 us; the launch traced here: 58.8 us
  Pallas kernels  55.9 us (95%)
  other arithmetic  2.83 us (5%)
    pallas_call x1, Pallas kernels, fast(): pl.pallas_call(functools.partial(kernel, chunks, lax.axis_size('energy'))...  55.9 us
    convert_element_type x1, other arithmetic, fast(): return pl.pallas_call(functools.partial(kernel, chunks, lax.axis_size('en...  2.83 us

profile of v1, /device:TPU:0, one launch (start us, length us, event | category | flops | bytes accessed | tf_op | source)
XLA Modules:
  0.0 58.8 jit_solution(17749339448528945972)
XLA Ops:
  0.0 55.9 %shard_map.64 = bf16[2,2,2,128,512]{4,3,2,1,0:T(8,128)(2,1)} custom-call(bf16[2,2,2,512,512]{4,3,2,1,0:T(8,128)(2,1)} %lesser.1, bf16[2,2,2,512,512]{4,3,2,1,0:T(8,128)(2,1)} %retarded.1, bf16[2,512,512]{2,1,0:T(8,128)(2,1)} %coupling.1, f32[2]{0:T(128)} %numbers.1, s32[2]{0:T(128)} %shifts.1, f32[2]{0:T(128)} %beside_weight.1), custom_call_target="tpu_custom_call" | custom-call | tf_op jit(solution)/shard_map/pallas_call | solution.py:405
  56.0 2.8 %convert_element_type.3 = f32[2,2,2,128,512]{4,3,2,1,0:T(8,128)} convert(bf16[2,2,2,128,512]{4,3,2,1,0:T(8,128)(2,1)} %shard_map.64) | non-fusion elementwise | flops 524288 | bytes 3145728 | tf_op jit(solution)/shard_map/convert_element_type | solution.py:433

commit v2 on v1

--- a/solution.py
+++ b/solution.py
@@ -197,19 +197,19 @@
         k, rows = blocks[b]
         return c_buf.at[k, rows, pl.ds(slot * cut, cut)]
 
+    w_in = [go(remote(w_buf.at[pl.ds(0, nf)], w_buf.at[pl.ds(nf, nf)], partner))]
+    for i in range(nf):
+        slot = 4 + 2 * (x if i == 0 else 1 - x)
+        w_in.append(go(remote(w_buf.at[i], w_buf.at[slot], across)))
+        w_in.append(go(remote(w_buf.at[i], w_buf.at[slot + 1], diagonal)))
     c_across = [go(remote(coupling.at[x, rows, columns_of[k]], block(4, b), across)) for b, (k, rows) in enumerate(blocks)]
+    c_near = [go(remote(coupling.at[i, :, columns_of[k]], part(nf + i, k), partner)) for i in range(nf) for k in range(chunks)]
     near, far, passed = {}, {}, {}
     for p, (s, c) in enumerate(pieces):
         for k in range(chunks):
             near[p, k] = go(remote(lesser.at[1 - core, s, c, :, columns_of[k]], green.at[p, k, near_slot], along), has_to)
             far[p, k] = go(remote(lesser.at[core, s, c, :, columns_of[k]], green.at[p, k, far_slot], along), has_to)
             passed[p, k] = remote(green.at[p, k, near_slot], green.at[p, k, pass_to], partner)
-    w_in = [go(remote(w_buf.at[pl.ds(0, nf)], w_buf.at[pl.ds(nf, nf)], partner))]
-    for i in range(nf):
-        slot = 4 + 2 * (x if i == 0 else 1 - x)
-        w_in.append(go(remote(w_buf.at[i], w_buf.at[slot], across)))
-        w_in.append(go(remote(w_buf.at[i], w_buf.at[slot + 1], diagonal)))
-    c_near = [go(remote(coupling.at[i, :, columns_of[k]], part(nf + i, k), partner)) for i in range(nf) for k in range(chunks)]
     for load in load_own[1] + load_own[2] + load_r:
         load.start()
 
@@ -254,17 +254,12 @@
         columns = slice(start * cut, stop * cut)
         return by_rows(left_buf[k, :, columns], c_buf[k, rows, columns])
 
-    halves = [slice(h * half, (h + 1) * half) for h in range(2)]
-    to_across = [remote(edge_own.at[h], edge_other.at[h], across) for h in range(2)]
-    to_beside = [remote(edge_own.at[h], near_own.at[h], opposite) for h in range(2)]
-    over_across = remote(near_own.at[1], near_other.at[1], across)
-    over_beside = remote(edge_other.at[0], near_other.at[0], opposite)
-    to_partner = {
-        (s, c, h): remote(comb.at[0, s, c, h], comb.at[1, s, c, h], partner)
-        for s in range(2)
-        for c in range(2)
-        for h in range(2)
-    }
+    halves = [pl.ds(h * half, half) for h in range(2)]
+    to_across = [remote(edge_own.at[:, columns], edge_other.at[:, columns], across) for columns in halves]
+    to_beside = [remote(edge_own.at[:, columns], near_own.at[:, columns], opposite) for columns in halves]
+    over_across = remote(near_own.at[:, halves[1]], near_other.at[:, halves[1]], across)
+    over_beside = remote(edge_other.at[:, halves[0]], near_other.at[:, halves[0]], opposite)
+    to_partner = {(m, c): remote(comb.at[0, m, c], comb.at[1, m, c], partner) for m in range(2) for c in range(2)}
     weight_outer, weight_edge = beside_weight[outer], beside_weight[edge]
     last = chunks - 1
 
@@ -301,13 +296,11 @@
         copy.wait_recv()
     left_side(0, 0, 6, 8)
     left_side(0, 1, 6, 8)
-    for h in range(2):
-        total = acc[0, :, halves[h]] + (right_side(0, 6, 8, halves[h]) + right_side(1, 6, 8, halves[h]))
-        edge_own[h] = total.astype(BF16)
-        go(to_across[h])
-        if h == 1:
-            go(to_beside[1])
-            go(to_beside[0])
+    edge_own[...] = (acc[0] + (right_side(0, 6, 8) + right_side(1, 6, 8))).astype(BF16)
+    go(to_across[0])
+    go(to_beside[1])
+    go(to_across[1])
+    go(to_beside[0])
 
     for load in load_own[1] + load_own[2] + load_r:
         load.wait()
@@ -326,12 +319,11 @@
     pass_on(1, 1)
     arrive(1, 1)
     left_side(1, 1, 0, 8)
-    for h in range(2):
-        total = acc[1, :, halves[h]] + right_side(last, 0, 8, halves[h])
-        own = edge_own[h].astype(F32)
-        comb[0, 0, 0, h] = (total + weight_outer * own).astype(BF16)
-        go(to_partner[0, 0, h])
-        acc[1, :, halves[h]] = own + weight_edge * total
+    total = acc[1] + right_side(last, 0, 8)
+    own = edge_own[...].astype(F32)
+    comb[0, 0, 0] = (total + weight_outer * own).astype(BF16)
+    go(to_partner[0, 0])
+    acc[1] = own + weight_edge * total
     to_beside[1].wait_recv()
     go(over_across)
     to_across[0].wait_recv()
@@ -341,42 +333,36 @@
     left_side(2, 0, 0, 8)
     acc[0] = right_side(0, 0, 8)
 
-    def project(n, m, c, h):
-        return jnp.dot(rows_of[n, m, c], comb[n, m, c, h], preferred_element_type=F32)
+    def project(n, m, c):
+        return jnp.dot(rows_of[n, m, c], comb[n, m, c], preferred_element_type=F32)
 
     to_beside[0].wait_recv()
-    for h in range(2):
-        comb[0, 1, 0, h] = (acc[1, :, halves[h]] + weight_edge * near_own[h].astype(F32)).astype(BF16)
-        go(to_partner[1, 0, h])
+    comb[0, 1, 0] = (acc[1] + weight_edge * near_own[...].astype(F32)).astype(BF16)
+    go(to_partner[1, 0])
     pass_on(2, 1)
     for n in range(2):
         for m in range(2):
-            for h in range(2):
-                if n == 1:
-                    to_partner[m, 0, h].wait_recv()
-                middle[n, m, :, halves[h]] = project(n, m, 0, h)
+            if n == 1:
+                to_partner[m, 0].wait_recv()
+            middle[n, m] = project(n, m, 0)
     to_across[1].wait_recv()
     arrive(2, 1)
     left_side(2, 1, 0, 8)
     over_across.wait_recv()
     over_beside.wait_recv()
-    for h in range(2):
-        total = acc[0, :, halves[h]] + right_side(last, 0, 8, halves[h])
-        other = edge_other[h].astype(F32)
-        comb[0, 0, 1, h] = (total + weight_outer * other).astype(BF16)
-        go(to_partner[0, 1, h])
-        comb[0, 1, 1, h] = (other + weight_edge * (total + near_other[h].astype(F32))).astype(BF16)
-        go(to_partner[1, 1, h])
+    total = acc[0] + right_side(last, 0, 8)
+    other = edge_other[...].astype(F32)
+    comb[0, 0, 1] = (total + weight_outer * other).astype(BF16)
+    go(to_partner[0, 1])
+    comb[0, 1, 1] = (other + weight_edge * (total + near_other[...].astype(F32))).astype(BF16)
+    go(to_partner[1, 1])
 
     stores = []
     for n, e in enumerate((core, 1 - core)):
         for m, s in enumerate((outer, edge)):
-            whole = []
-            for h in range(2):
-                if n == 1:
-                    to_partner[m, 1, h].wait_recv()
-                whole.append((middle[n, m, :, halves[h]] + project(n, m, 1, h)).astype(BF16))
-            both = jnp.concatenate(whole, axis=1)
+            if n == 1:
+                to_partner[m, 1].wait_recv()
+            both = (middle[n, m] + project(n, m, 1)).astype(BF16)
             real, imag = both[:rows], both[rows:]
             sides = jnp.concatenate(
                 [jnp.concatenate([real, imag], axis=1), jnp.concatenate([imag, -real], axis=1)], axis=0
@@ -399,7 +385,7 @@
     chunks = 2
     cut = size // chunks
     rows = size // 4
-    copies = chunks * (2 * BLOCKS + 3 * PIECES + 2 + nf) + 1 + 2 * nf + 14
+    copies = chunks * (2 * BLOCKS + 3 * PIECES + 2 + nf) + 1 + 2 * nf + 10
     loads = PIECES * chunks + nf * chunks + 8
     anywhere = pl.BlockSpec(memory_space=pl.ANY)
     return pl.pallas_call(
@@ -414,11 +400,11 @@
             pltpu.VMEM((2, 2, size, 2 * size), BF16),
             pltpu.VMEM((chunks, size, 4 * nf * cut), BF16),
             pltpu.VMEM((2, size, size), F32),
-            pltpu.VMEM((2, size, size // 2), BF16),
-            pltpu.VMEM((2, size, size // 2), BF16),
-            pltpu.VMEM((2, size, size // 2), BF16),
-            pltpu.VMEM((2, size, size // 2), BF16),
-            pltpu.VMEM((2, 2, 2, 2, size, size // 2), BF16),
+            pltpu.VMEM((size, size), BF16),
+            pltpu.VMEM((size, size), BF16),
+            pltpu.VMEM((size, size), BF16),
+            pltpu.VMEM((size, size), BF16),
+            pltpu.VMEM((2, 2, 2, size, size), BF16),
             pltpu.VMEM((2, 2, 2, 2 * rows, size), BF16),
             pltpu.VMEM((2, 2, 2 * rows, size), F32),
             pltpu.VMEM((2, 2, 2, rows, size), BF16),

time: 58.9 us -> 52.3 us (0.89)
  Pallas kernels: 55.9 us -> 49.3 us
    pallas_call x1, Pallas kernels: 55.9 us -> 49.3 us  [fast(): pl.pallas_call(functools.partial(kernel, chunks, lax.axis_size('energy'))...]
where the time goes in v2:
time: 52.3 us; the launch traced here: 52.1 us
  Pallas kernels  49.3 us (94%)
  other arithmetic  2.83 us (5%)
    pallas_call x1, Pallas kernels, fast(): pl.pallas_call(functools.partial(kernel, chunks, lax.axis_size('energy'))...  49.3 us
    convert_element_type x1, other arithmetic, fast(): return pl.pallas_call(functools.partial(kernel, chunks, lax.axis_size('en...  2.83 us

profile of v2, /device:TPU:0, one launch (start us, length us, event | category | flops | bytes accessed | tf_op | source)
XLA Modules:
  0.0 52.1 jit_solution(6532768925683841648)
XLA Ops:
  0.0 49.3 %shard_map.64 = bf16[2,2,2,128,512]{4,3,2,1,0:T(8,128)(2,1)} custom-call(bf16[2,2,2,512,512]{4,3,2,1,0:T(8,128)(2,1)} %lesser.1, bf16[2,2,2,512,512]{4,3,2,1,0:T(8,128)(2,1)} %retarded.1, bf16[2,512,512]{2,1,0:T(8,128)(2,1)} %coupling.1, f32[2]{0:T(128)} %numbers.1, s32[2]{0:T(128)} %shifts.1, f32[2]{0:T(128)} %beside_weight.1), custom_call_target="tpu_custom_call" | custom-call | tf_op jit(solution)/shard_map/pallas_call | solution.py:391
  49.3 2.8 %convert_element_type.3 = f32[2,2,2,128,512]{4,3,2,1,0:T(8,128)} convert(bf16[2,2,2,128,512]{4,3,2,1,0:T(8,128)(2,1)} %shard_map.64) | non-fusion elementwise | flops 524288 | bytes 3145728 | tf_op jit(solution)/shard_map/convert_element_type | solution.py:419

commit v3 on v2

v3 whole, which is shorter than its diff:
```python
import functools
import jax
import jax.numpy as jnp
from jax import lax
from jax.experimental import pallas as pl
from jax.experimental.pallas import tpu as pltpu
from jax.sharding import PartitionSpec as P

OFFMAX = 2
UNROLL = 8
PIECES = 3
BLOCKS = 8
GROUPS = 14
MESH = pl.DeviceIdType.MESH
F32 = jnp.float32
BF16 = jnp.bfloat16


def with_halo(block, sides, width):
    for axis, dim in sides:
        count = lax.axis_size(axis)
        forward = [(i, i + 1) for i in range(count - 1)]
        backward = [(target, source) for source, target in forward]
        low = lax.ppermute(
            lax.slice_in_dim(block, block.shape[dim] - width, None, axis=dim), axis, forward
        )
        high = lax.ppermute(lax.slice_in_dim(block, 0, width, axis=dim), axis, backward)
        block = jnp.concatenate([low, block, high], axis=dim)
    return block


def general(lesser, retarded, coupling, occupations, offsets, intersection):
    freq_count = lax.axis_size("freq")
    row_count = lesser.shape[-1] // freq_count
    row_first = lax.axis_index("freq") * row_count
    padded = with_halo(lesser, (("energy", 0),), OFFMAX)
    energy_count = lesser.shape[0]
    positions = jnp.arange(energy_count, dtype=jnp.int32)[None, :] + OFFMAX
    lower_green = jnp.take(padded, positions - offsets[:, None], axis=0)
    upper_green = jnp.take(padded, positions + offsets[:, None], axis=0)
    scale = occupations[:, None, None, None, None, None]
    mixture = (
        scale * lower_green.astype(F32) + (scale + 1.0) * upper_green.astype(F32)
    ).astype(BF16)
    real_green = retarded[:, :, 0]
    imag_green = retarded[:, :, 1]
    real_rows = lax.dynamic_slice_in_dim(real_green, row_first, row_count, 2)
    imag_rows = lax.dynamic_slice_in_dim(imag_green, row_first, row_count, 2)
    left_product = jnp.einsum(
        "fri,fescij->fescrj", coupling, mixture, preferred_element_type=F32
    ).astype(BF16)
    self_energy = lax.psum_scatter(
        jnp.einsum(
            "fescrj,fkj->resck", left_product, coupling, preferred_element_type=F32
        ).astype(BF16),
        "freq",
        scatter_dimension=0,
        tiled=True,
    )
    beside_all = with_halo(self_energy, (("slab", 2),), 1)
    beside = beside_all[:, :, :-2].astype(F32) + beside_all[:, :, 2:].astype(F32)
    total = self_energy.astype(F32) + intersection[None, None, :, None, None] * beside
    combined = total.astype(BF16)
    real_self = combined[:, :, :, 0]
    imag_self = combined[:, :, :, 1]

    def by_transpose(left_side, right_side):
        return jnp.einsum("resj,eskj->resk", left_side, right_side, preferred_element_type=F32)

    real_part = by_transpose(real_self, real_green) + by_transpose(imag_self, imag_green)
    imag_part = by_transpose(imag_self, real_green) - by_transpose(real_self, imag_green)
    product = jnp.stack([real_part, imag_part], axis=3).astype(BF16)
    y_piece = lax.all_gather(product, "freq", axis=0, tiled=True)
    real_piece = y_piece[:, :, :, 0]
    imag_piece = y_piece[:, :, :, 1]

    def plain_product(left_side, right_side):
        return jnp.einsum("esrm,mesk->esrk", left_side, right_side, preferred_element_type=F32)

    out_real = plain_product(real_rows, real_piece) - plain_product(imag_rows, imag_piece)
    out_imag = plain_product(real_rows, imag_piece) + plain_product(imag_rows, real_piece)
    return jnp.stack([out_real, out_imag], axis=2)


def by_rows(a, b):
    return lax.dot_general(a, b, (((1,), (1,)), ((), ())), preferred_element_type=F32)


def kernel(
    chunks, energies,
    lesser, retarded, coupling, numbers, shifts, beside_weight, out,
    green, c_buf, w_tile, w_buf, r_buf, left_buf, acc, edge_own, edge_other, near_own, near_other,
    comb, rows_of, middle,
    local_sem, send_sem, recv_sem,
):
    nf, size, _ = coupling.shape
    cut = size // chunks
    half = size // 2
    x, q, z = lax.axis_index("slab"), lax.axis_index("freq"), lax.axis_index("energy")
    y, core = q // 2, q % 2
    outer, edge = x, 1 - x
    partner = {"freq": 2 * y + 1 - core}
    across = {"freq": 2 * (1 - y) + core}
    diagonal = {"freq": 2 * (1 - y) + 1 - core}
    opposite = {"slab": 1 - x}
    has_low, has_high = z > 0, z < energies - 1
    below = {"energy": jnp.maximum(z - 1, 0)}
    above = {"energy": jnp.minimum(z + 1, energies - 1)}
    first = core == 0
    second = core == 1
    has_to = jnp.logical_or(jnp.logical_and(first, has_high), jnp.logical_and(second, has_low))
    has_from = jnp.logical_or(jnp.logical_and(first, has_low), jnp.logical_and(second, has_high))
    along = {"energy": jnp.clip(z + 1 - 2 * core, 0, energies - 1)}

    barrier = pltpu.get_barrier_semaphore()
    peers = [(None, partner), (None, across), (None, diagonal), (None, opposite), (has_low, below), (has_high, above)]

    def under(condition, action):
        if condition is None:
            action()
        else:
            pl.when(condition)(action)

    for condition, peer in peers:
        under(condition, lambda peer=peer: pl.semaphore_signal(barrier, inc=1, device_id=peer, device_id_type=MESH))

    count = [0]
    groups = []

    def group(total, condition=None):
        groups.append((total, condition))
        return len(groups) - 1, condition

    def remote(src, dst, peer, kind):
        n = count[0]
        count[0] += 1
        copy = pltpu.make_async_remote_copy(
            src_ref=src, dst_ref=dst, send_sem=send_sem.at[kind[0]], recv_sem=recv_sem.at[n],
            device_id=peer, device_id_type=MESH,
        )
        return copy, kind[1]

    def go(pair):
        under(pair[1], pair[0].start)
        return pair

    def came(pair):
        pair[0].wait_recv()

    pieces = [(edge, y), (outer, y), (outer, 1 - y)]
    near_slot, far_slot, own_slot = 2 * core, 2 * core + 1, 2 - 2 * core
    passed_slot, pass_to = 3 - 2 * core, 1 + 2 * core
    columns_of = [pl.ds(k * cut, cut) for k in range(chunks)]
    load_c = pltpu.make_async_copy(coupling, c_buf.at[pl.ds(0, nf)], local_sem.at[0])
    load_r = pltpu.make_async_copy(retarded, r_buf, local_sem.at[1])
    load_own = [
        pltpu.make_async_copy(lesser.at[1 - core, s, c], green.at[p, own_slot], local_sem.at[2 + p])
        for p, (s, c) in enumerate(pieces)
    ]
    load_c.start()
    load_own[0].start()

    for i in range(nf):
        number, shift = numbers[i], shifts[i]
        none = jnp.float32(0.0)
        row = [
            jnp.where(shift == 1, number, none),
            jnp.where(shift == 2, number, none),
            jnp.where(shift == 1, number + 1.0, none),
            jnp.where(shift == 2, number + 1.0, none),
        ]
        for j in range(4):
            w_tile[0, 4 * i + j : 4 * i + j + 1, :] = jnp.full((1, 128), row[j], F32)

    def zero(p, slot):
        green[p, slot] = jnp.zeros((size, size), BF16)

    def fill(p):
        pl.when(jnp.logical_not(has_from))(lambda: zero(p, near_slot))
        pl.when(jnp.logical_not(has_from))(lambda: zero(p, far_slot))
        pl.when(jnp.logical_not(has_to))(lambda: zero(p, passed_slot))

    greeted = 4 + sum(condition.astype(jnp.int32) for condition in (has_low, has_high))
    pl.semaphore_wait(barrier, greeted)

    depth = size // BLOCKS
    rows_at = [pl.ds(b * depth, depth) for b in range(BLOCKS)]
    relays = BLOCKS - 1
    for_w = group(w_tile.at[pl.ds(0, 3)])
    w_in = [go(remote(w_tile.at[0], w_tile.at[d + 1], peer, for_w)) for d, peer in enumerate((partner, across, diagonal))]
    for_across = group(c_buf.at[4])
    for_direct = group(c_buf.at[4, rows_at[relays]])
    c_across = [go(remote(coupling.at[x, rows], c_buf.at[4, rows], across, for_across)) for rows in rows_at]
    c_direct = go(remote(coupling.at[1 - x, rows_at[relays]], c_buf.at[6, rows_at[relays]], across, for_direct))
    for_z = group(green.at[:, pl.ds(0, 2)], has_to)
    for_passed = group(green.at[:, 0], has_from)
    near, far, passed = {}, {}, {}
    for_near = group(coupling)
    for p, (s, c) in enumerate(pieces):
        for k, columns in enumerate(columns_of):
            near[p, k] = go(remote(lesser.at[1 - core, s, c, :, columns], green.at[p, near_slot, :, columns], along, for_z))
            far[p, k] = go(remote(lesser.at[core, s, c, :, columns], green.at[p, far_slot, :, columns], along, for_z))
            passed[p, k] = remote(green.at[p, near_slot, :, columns], green.at[p, pass_to, :, columns], partner, for_passed)
        if p == 0:
            c_near = go(remote(coupling, c_buf.at[pl.ds(nf, nf)], partner, for_near))
    for load in load_own[1:] + [load_r]:
        load.start()

    for_relay, for_far, for_rest = group(c_buf.at[4, pl.ds(0, relays * depth)]), group(c_buf.at[4]), group(c_buf.at[6])
    relayed = [remote(c_buf.at[4, rows], c_buf.at[6, rows], opposite, for_relay) for rows in rows_at[:relays]]
    whole_halves = [pl.ds(h * half, half) for h in range(2)]
    c_far = [remote(c_buf.at[4, rows], c_buf.at[5, rows], partner, for_far) for rows in whole_halves]
    c_rest = [remote(c_buf.at[6, rows], c_buf.at[7, rows], partner, for_rest) for rows in whole_halves]

    def pump(b):
        came(c_across[b])
        if b < relays:
            go(relayed[b])
        if b == BLOCKS // 2 - 1:
            go(c_far[0])
        if b == BLOCKS - 1:
            go(c_far[1])

    def rest(h):
        for b in range(h * BLOCKS // 2, (h + 1) * BLOCKS // 2):
            came(relayed[b] if b < relays else c_direct)
        go(c_rest[h])

    def pass_on(p, k):
        pl.when(has_from)(near[p, k][0].wait_recv)
        go(passed[p, k])

    def arrive(p, k):
        pl.when(has_from)(far[p, k][0].wait_recv)
        pl.when(has_to)(passed[p, k][0].wait_recv)

    def spread():
        for slot in range(4 * nf):
            source = slot // 2 if slot < 4 else 2 + slot % 2
            for i in range(4):
                if slot < 4:
                    row = w_tile[source, 4 * (slot % 2) + i : 4 * (slot % 2) + i + 1]
                else:
                    pair = (w_tile[source, i : i + 1], w_tile[source, 4 + i : 5 + i])
                    row = jnp.where((x == 0) == (slot < 6), pair[0], pair[1])
                wide = jnp.broadcast_to(row, (16, 128)).astype(BF16)
                w_buf[slot, i] = jnp.concatenate([wide] * (size // 128), axis=1)

    def mixture(p, columns, f):
        width = columns.stop - columns.start

        def term(i):
            block = green[p, i, :, columns].reshape(size // 16, 16, width)
            return w_buf[f, i, :, columns][None] * block

        return ((term(0) + term(1)) + (term(2) + term(3))).reshape(size, width)

    def left_side(p, columns, start, stop):
        def product(f, carry):
            left = jnp.dot(c_buf[f], mixture(p, columns, f), preferred_element_type=F32)
            left_buf[f, :, columns] = left.astype(BF16)
            return carry

        lax.fori_loop(start, stop, product, 0, unroll=min(UNROLL, stop - start))

    def right_side(columns, start, stop):
        def beside(ref):
            return jnp.concatenate([ref[f, :, columns] for f in range(start, stop)], axis=1)

        return by_rows(beside(left_buf), beside(c_buf))

    part = [slice(k * cut, (k + 1) * cut) for k in range(chunks)]
    full = slice(0, size)
    halves = whole_halves
    for_edge, for_beside = group(edge_own), group(edge_own)
    to_across = [remote(edge_own.at[:, columns], edge_other.at[:, columns], across, for_edge) for columns in halves]
    to_beside = [remote(edge_own.at[:, columns], near_own.at[:, columns], opposite, for_beside) for columns in halves]
    over_across = remote(near_own.at[:, halves[1]], near_other.at[:, halves[1]], across, group(near_own.at[:, halves[1]]))
    over_beside = remote(edge_other.at[:, halves[0]], near_other.at[:, halves[0]], opposite, group(near_own.at[:, halves[1]]))
    for_comb = group(comb.at[0])
    to_partner = {
        (m, c): remote(comb.at[0, m, c], comb.at[1, m, c], partner, for_comb) for m in range(2) for c in range(2)
    }
    weight_outer, weight_edge = beside_weight[outer], beside_weight[edge]

    fill(0)
    pump(0)
    pump(1)
    pass_on(0, 0)
    pump(2)
    pump(3)
    for copy in w_in:
        came(copy)
    spread()
    load_c.wait()
    load_own[0].wait()
    came(c_near)
    arrive(0, 0)
    left_side(0, part[0], 0, 2)
    pump(4)
    left_side(0, part[0], 2, 4)
    pump(5)
    acc[0] = right_side(part[0], 0, 4)
    pass_on(0, 1)
    pump(6)
    rest(0)
    pump(7)
    arrive(0, 1)
    left_side(0, part[1], 0, 4)
    acc[0] += right_side(part[1], 0, 4)
    for copy in c_far:
        came(copy)
    left_side(0, full, 4, 6)
    rest(1)
    acc[0] += right_side(full, 4, 6)
    pass_on(1, 0)
    for copy in c_rest:
        came(copy)
    left_side(0, full, 6, 8)
    edge_own[...] = (acc[0] + right_side(full, 6, 8)).astype(BF16)
    go(to_across[0])
    go(to_beside[1])
    go(to_across[1])
    go(to_beside[0])

    fill(1)
    fill(2)
    for load in load_own[1:] + [load_r]:
        load.wait()
    rows = size // 4
    mine = pl.ds(pl.multiple_of(q * rows, rows), rows)
    here = y == 0
    for n, e in enumerate((core, 1 - core)):
        for m, s in enumerate((outer, edge)):
            real, imag = r_buf[e, s, 0, mine], r_buf[e, s, 1, mine]
            rows_of[n, m, 0] = jnp.concatenate([jnp.where(here, real, -imag), jnp.where(here, imag, real)], axis=0)
            rows_of[n, m, 1] = jnp.concatenate([jnp.where(here, -imag, real), jnp.where(here, real, imag)], axis=0)

    arrive(1, 0)
    left_side(1, part[0], 0, 8)
    acc[1] = right_side(part[0], 0, 8)
    pass_on(1, 1)
    arrive(1, 1)
    left_side(1, part[1], 0, 8)
    total = acc[1] + right_side(part[1], 0, 8)
    own = edge_own[...].astype(F32)
    comb[0, 0, 0] = (total + weight_outer * own).astype(BF16)
    go(to_partner[0, 0])
    acc[1] = own + weight_edge * total
    came(to_beside[1])
    go(over_across)
    came(to_across[0])
    go(over_beside)
    pass_on(2, 0)
    arrive(2, 0)
    left_side(2, part[0], 0, 8)
    acc[0] = right_side(part[0], 0, 8)

    def project(n, m, c):
        return jnp.dot(rows_of[n, m, c], comb[n, m, c], preferred_element_type=F32)

    came(to_beside[0])
    comb[0, 1, 0] = (acc[1] + weight_edge * near_own[...].astype(F32)).astype(BF16)
    go(to_partner[1, 0])
    pass_on(2, 1)
    for n in range(2):
        for m in range(2):
            if n == 1:
                came(to_partner[m, 0])
            middle[n, m] = project(n, m, 0)
    came(to_across[1])
    arrive(2, 1)
    left_side(2, part[1], 0, 8)
    acc[0] += right_side(part[1], 0, 8)
    comb[0, 0, 1] = (acc[0] + weight_outer * edge_other[...].astype(F32)).astype(BF16)
    go(to_partner[0, 1])

    def finish(n, m):
        e, s = (core, 1 - core)[n], (outer, edge)[m]
        if n == 1:
            came(to_partner[m, 1])
        both = (middle[n, m] + project(n, m, 1)).astype(BF16)
        real, imag = both[:rows], both[rows:]
        sides = jnp.concatenate(
            [jnp.concatenate([real, imag], axis=1), jnp.concatenate([imag, -real], axis=1)], axis=0
        )
        updated = by_rows(sides, jnp.concatenate([r_buf[e, s, 0], r_buf[e, s, 1]], axis=1))
        out[e, s, 0] = updated[:rows]
        out[e, s, 1] = updated[rows:]

    finish(0, 0)
    came(over_across)
    came(over_beside)
    around = acc[0] + near_other[...].astype(F32)
    comb[0, 1, 1] = (edge_other[...].astype(F32) + weight_edge * around).astype(BF16)
    go(to_partner[1, 1])
    finish(1, 0)
    finish(0, 1)
    finish(1, 1)

    for n, (total, condition) in enumerate(groups):
        done = pltpu.make_async_remote_copy(
            src_ref=total, dst_ref=total, send_sem=send_sem.at[n], recv_sem=recv_sem.at[0],
            device_id=partner, device_id_type=MESH,
        )
        under(condition, done.wait_send)


def fast(lesser, retarded, coupling, occupations, offsets, intersection):
    nf, size, _ = coupling.shape
    chunks = 2
    rows = size // 4
    arrivals = 3 + 1 + BLOCKS + 1 + (BLOCKS - 1) + 4 + 3 * PIECES * chunks + 6 + 4
    anywhere = pl.BlockSpec(memory_space=pl.ANY)
    return pl.pallas_call(
        functools.partial(kernel, chunks, lax.axis_size("energy")),
        out_shape=pltpu.VMEM((2, 2, 2, rows, size), F32),
        in_specs=[anywhere] * 3 + [pl.BlockSpec(memory_space=pltpu.SMEM)] * 3,
        out_specs=pl.BlockSpec(memory_space=pltpu.VMEM),
        scratch_shapes=[
            pltpu.VMEM((PIECES, 4, size, size), BF16),
            pltpu.VMEM((4 * nf, size, size), BF16),
            pltpu.VMEM((4, 8, 128), F32),
            pltpu.VMEM((4 * nf, 4, 16, size), BF16),
            pltpu.VMEM((2, 2, 2, size, size), BF16),
            pltpu.VMEM((4 * nf, size, size), BF16),
            pltpu.VMEM((2, size, size), F32),
            pltpu.VMEM((size, size), BF16),
            pltpu.VMEM((size, size), BF16),
            pltpu.VMEM((size, size), BF16),
            pltpu.VMEM((size, size), BF16),
            pltpu.VMEM((2, 2, 2, size, size), BF16),
            pltpu.VMEM((2, 2, 2, 2 * rows, size), BF16),
            pltpu.VMEM((2, 2, 2 * rows, size), F32),
            pltpu.SemaphoreType.DMA((2 + PIECES,)),
            pltpu.SemaphoreType.DMA((GROUPS,)),
            pltpu.SemaphoreType.DMA((arrivals,)),
        ],
        compiler_params=pltpu.CompilerParams(
            collective_id=0, has_side_effects=True, vmem_limit_bytes=60 << 20
        ),
    )(lesser, retarded, coupling, occupations, offsets, intersection)


def solution(mesh):
    def shards(lesser, retarded, *rest):
        fits = (
            (mesh.shape["slab"], mesh.shape["freq"]) == (2, 4)
            and lesser.shape[:2] == (2, 2)
            and lesser.shape[-1] == 512
            and rest[0].shape[0] == 2
        )
        return (fast if fits else general)(lesser, retarded, *rest)

    return jax.shard_map(
        shards,
        mesh=mesh,
        in_specs=(
            P("energy", "slab", None, None, None),
            P("energy", "slab", None, None, None),
            P("freq", None, None),
            P("freq"),
            P("freq"),
            P("slab"),
        ),
        out_specs=P("energy", "slab", None, "freq", None),
        check_vma=False,
    )
```

time: 52.3 us -> 48 us (0.918)
  other arithmetic: 2.83 us -> 0 us
  Pallas kernels: 49.3 us -> 46.5 us
  local copies, waits for them, and re-layouts: 0 us -> 1.32 us
    convert_element_type x1 -> x0, other arithmetic: 2.83 us -> none  [fast(): return pl.pallas_call(functools.partial(kernel, chunks, lax.axis_size('en...]
    pallas_call x1, Pallas kernels: 49.3 us -> 46.5 us  [fast(): pl.pallas_call(functools.partial(kernel, chunks, lax.axis_size('energy'))...]
    unnamed x0 -> x1, local copies, waits for them, and re-layouts: none -> 1.32 us
where the time goes in v3:
time: 48 us; the launch traced here: 47.9 us
  Pallas kernels  46.5 us (97%)
  local copies, waits for them, and re-layouts  1.32 us (3%)
    pallas_call x1, Pallas kernels, fast(): pl.pallas_call(functools.partial(kernel, chunks, lax.axis_size('energy'))...  46.5 us
    unnamed x1, local copies, waits for them, and re-layouts  1.32 us

profile of v3, /device:TPU:0, one launch (start us, length us, event | category | flops | bytes accessed | tf_op | source)
XLA Modules:
  0.0 47.9 jit_solution(3556805690590750939)
XLA Ops:
  0.0 46.5 %shard_map.64 = f32[2,2,2,128,512]{4,3,2,1,0:T(8,128)S(1)} custom-call(bf16[2,2,2,512,512]{4,3,2,1,0:T(8,128)(2,1)} %lesser.1, bf16[2,2,2,512,512]{4,3,2,1,0:T(8,128)(2,1)} %retarded.1, bf16[2,512,512]{2,1,0:T(8,128)(2,1)} %coupling.1, f32[2]{0:T(128)} %numbers.1, s32[2]{0:T(128)} %shifts.1, f32[2]{0:T(128)} %beside_weight.1), custom_call_target="tpu_custom_call" | custom-call | tf_op jit(solution)/shard_map/pallas_call | solution.py:415
  46.5 1.3 %copy.8 = f32[2,2,2,128,512]{4,3,2,1,0:T(8,128)} copy(f32[2,2,2,128,512]{4,3,2,1,0:T(8,128)S(1)} %shard_map.64) | data formatting | bytes 4194304

commit v4 on v3

--- a/solution.py
+++ b/solution.py
@@ -9,7 +9,8 @@
 OFFMAX = 2
 UNROLL = 8
 PIECES = 3
-BLOCKS = 8
+RELAYS = (96, 96, 96, 64, 64, 32)
+EARLY = 3
 GROUPS = 14
 MESH = pl.DeviceIdType.MESH
 F32 = jnp.float32
@@ -87,33 +88,30 @@
 
 
 def kernel(
-    chunks, energies,
+    energies,
     lesser, retarded, coupling, numbers, shifts, beside_weight, out,
     green, c_buf, w_tile, w_buf, r_buf, left_buf, acc, edge_own, edge_other, near_own, near_other,
     comb, rows_of, middle,
     local_sem, send_sem, recv_sem,
 ):
     nf, size, _ = coupling.shape
-    cut = size // chunks
     half = size // 2
     x, q, z = lax.axis_index("slab"), lax.axis_index("freq"), lax.axis_index("energy")
     y, core = q // 2, q % 2
     outer, edge = x, 1 - x
     partner = {"freq": 2 * y + 1 - core}
     across = {"freq": 2 * (1 - y) + core}
-    diagonal = {"freq": 2 * (1 - y) + 1 - core}
     opposite = {"slab": 1 - x}
     has_low, has_high = z > 0, z < energies - 1
-    below = {"energy": jnp.maximum(z - 1, 0)}
-    above = {"energy": jnp.minimum(z + 1, energies - 1)}
     first = core == 0
     second = core == 1
     has_to = jnp.logical_or(jnp.logical_and(first, has_high), jnp.logical_and(second, has_low))
     has_from = jnp.logical_or(jnp.logical_and(first, has_low), jnp.logical_and(second, has_high))
     along = {"energy": jnp.clip(z + 1 - 2 * core, 0, energies - 1)}
+    behind = {"energy": jnp.clip(z - 1 + 2 * core, 0, energies - 1)}
 
     barrier = pltpu.get_barrier_semaphore()
-    peers = [(None, partner), (None, across), (None, diagonal), (None, opposite), (has_low, below), (has_high, above)]
+    peers = [(None, partner), (None, across), (None, opposite), (has_from, behind)]
 
     def under(condition, action):
         if condition is None:
@@ -150,7 +148,7 @@
     pieces = [(edge, y), (outer, y), (outer, 1 - y)]
     near_slot, far_slot, own_slot = 2 * core, 2 * core + 1, 2 - 2 * core
     passed_slot, pass_to = 3 - 2 * core, 1 + 2 * core
-    columns_of = [pl.ds(k * cut, cut) for k in range(chunks)]
+    parts = [slice(0, half), slice(half, size)]
     load_c = pltpu.make_async_copy(coupling, c_buf.at[pl.ds(0, nf)], local_sem.at[0])
     load_r = pltpu.make_async_copy(retarded, r_buf, local_sem.at[1])
     load_own = [
@@ -180,24 +178,25 @@
         pl.when(jnp.logical_not(has_from))(lambda: zero(p, far_slot))
         pl.when(jnp.logical_not(has_to))(lambda: zero(p, passed_slot))
 
-    greeted = 4 + sum(condition.astype(jnp.int32) for condition in (has_low, has_high))
-    pl.semaphore_wait(barrier, greeted)
-
-    depth = size // BLOCKS
-    rows_at = [pl.ds(b * depth, depth) for b in range(BLOCKS)]
-    relays = BLOCKS - 1
+    pl.semaphore_wait(barrier, 3 + has_to.astype(jnp.int32))
+
+    starts = [sum(RELAYS[:b]) for b in range(len(RELAYS) + 1)]
+    rows_at = [pl.ds(start, depth) for start, depth in zip(starts, RELAYS)]
+    kept = pl.ds(starts[-1], size - starts[-1])
+    staged = [pl.ds(0, starts[EARLY]), pl.ds(starts[EARLY], size - starts[EARLY])]
     for_w = group(w_tile.at[pl.ds(0, 3)])
-    w_in = [go(remote(w_tile.at[0], w_tile.at[d + 1], peer, for_w)) for d, peer in enumerate((partner, across, diagonal))]
+    w_in = [go(remote(w_tile.at[0], w_tile.at[d + 1], peer, for_w)) for d, peer in enumerate((partner, across))]
+    w_on = remote(w_tile.at[2], w_tile.at[3], partner, for_w)
     for_across = group(c_buf.at[4])
-    for_direct = group(c_buf.at[4, rows_at[relays]])
-    c_across = [go(remote(coupling.at[x, rows], c_buf.at[4, rows], across, for_across)) for rows in rows_at]
-    c_direct = go(remote(coupling.at[1 - x, rows_at[relays]], c_buf.at[6, rows_at[relays]], across, for_direct))
+    for_direct = group(c_buf.at[4, kept])
+    c_across = [go(remote(coupling.at[x, rows], c_buf.at[4, rows], across, for_across)) for rows in rows_at + [kept]]
+    c_direct = go(remote(coupling.at[1 - x, kept], c_buf.at[6, kept], across, for_direct))
     for_z = group(green.at[:, pl.ds(0, 2)], has_to)
     for_passed = group(green.at[:, 0], has_from)
     near, far, passed = {}, {}, {}
     for_near = group(coupling)
     for p, (s, c) in enumerate(pieces):
-        for k, columns in enumerate(columns_of):
+        for k, columns in enumerate(parts):
             near[p, k] = go(remote(lesser.at[1 - core, s, c, :, columns], green.at[p, near_slot, :, columns], along, for_z))
             far[p, k] = go(remote(lesser.at[core, s, c, :, columns], green.at[p, far_slot, :, columns], along, for_z))
             passed[p, k] = remote(green.at[p, near_slot, :, columns], green.at[p, pass_to, :, columns], partner, for_passed)
@@ -206,24 +205,23 @@
     for load in load_own[1:] + [load_r]:
         load.start()
 
-    for_relay, for_far, for_rest = group(c_buf.at[4, pl.ds(0, relays * depth)]), group(c_buf.at[4]), group(c_buf.at[6])
-    relayed = [remote(c_buf.at[4, rows], c_buf.at[6, rows], opposite, for_relay) for rows in rows_at[:relays]]
-    whole_halves = [pl.ds(h * half, half) for h in range(2)]
-    c_far = [remote(c_buf.at[4, rows], c_buf.at[5, rows], partner, for_far) for rows in whole_halves]
-    c_rest = [remote(c_buf.at[6, rows], c_buf.at[7, rows], partner, for_rest) for rows in whole_halves]
+    for_relay, for_far, for_rest = group(c_buf.at[4, pl.ds(0, starts[-1])]), group(c_buf.at[4]), group(c_buf.at[6])
+    relayed = [remote(c_buf.at[4, rows], c_buf.at[6, rows], opposite, for_relay) for rows in rows_at]
+    c_far = [remote(c_buf.at[4, rows], c_buf.at[5, rows], partner, for_far) for rows in staged]
+    c_rest = [remote(c_buf.at[6, rows], c_buf.at[7, rows], partner, for_rest) for rows in staged]
 
     def pump(b):
         came(c_across[b])
-        if b < relays:
+        if b < len(relayed):
             go(relayed[b])
-        if b == BLOCKS // 2 - 1:
+        if b == EARLY - 1:
             go(c_far[0])
-        if b == BLOCKS - 1:
+        if b == len(relayed):
             go(c_far[1])
 
     def rest(h):
-        for b in range(h * BLOCKS // 2, (h + 1) * BLOCKS // 2):
-            came(relayed[b] if b < relays else c_direct)
+        for copy in (relayed[EARLY:] + [c_direct]) if h else relayed[:EARLY]:
+            came(copy)
         go(c_rest[h])
 
     def pass_on(p, k):
@@ -269,45 +267,46 @@
 
         return by_rows(beside(left_buf), beside(c_buf))
 
-    part = [slice(k * cut, (k + 1) * cut) for k in range(chunks)]
     full = slice(0, size)
-    halves = whole_halves
+    halves = [pl.ds(h * half, half) for h in range(2)]
     for_edge, for_beside = group(edge_own), group(edge_own)
     to_across = [remote(edge_own.at[:, columns], edge_other.at[:, columns], across, for_edge) for columns in halves]
     to_beside = [remote(edge_own.at[:, columns], near_own.at[:, columns], opposite, for_beside) for columns in halves]
-    over_across = remote(near_own.at[:, halves[1]], near_other.at[:, halves[1]], across, group(near_own.at[:, halves[1]]))
-    over_beside = remote(edge_other.at[:, halves[0]], near_other.at[:, halves[0]], opposite, group(near_own.at[:, halves[1]]))
+    for_over, for_under = group(near_own.at[:, halves[1]]), group(near_own.at[:, halves[1]])
+    over_across = [remote(near_own.at[rows, halves[1]], near_other.at[rows, halves[1]], across, for_over) for rows in halves]
+    over_beside = [remote(edge_other.at[rows, halves[0]], near_other.at[rows, halves[0]], opposite, for_under) for rows in halves]
     for_comb = group(comb.at[0])
-    to_partner = {
-        (m, c): remote(comb.at[0, m, c], comb.at[1, m, c], partner, for_comb) for m in range(2) for c in range(2)
-    }
+    to_partner = {(m, c): remote(comb.at[0, m, c], comb.at[1, m, c], partner, for_comb) for m, c in ((0, 0), (1, 0), (0, 1))}
+    last_to_partner = [remote(comb.at[0, 1, 1, rows], comb.at[1, 1, 1, rows], partner, for_comb) for rows in halves]
     weight_outer, weight_edge = beside_weight[outer], beside_weight[edge]
 
     fill(0)
+    came(w_in[1])
+    go(w_on)
     pump(0)
+    pass_on(0, 0)
     pump(1)
-    pass_on(0, 0)
-    pump(2)
-    pump(3)
-    for copy in w_in:
-        came(copy)
+    came(w_in[0])
+    came(w_on)
     spread()
     load_c.wait()
     load_own[0].wait()
     came(c_near)
     arrive(0, 0)
-    left_side(0, part[0], 0, 2)
+    left_side(0, parts[0], 0, 2)
+    pump(2)
+    left_side(0, parts[0], 2, 4)
+    pump(3)
+    acc[0] = right_side(parts[0], 0, 4)
     pump(4)
-    left_side(0, part[0], 2, 4)
+    pass_on(0, 1)
     pump(5)
-    acc[0] = right_side(part[0], 0, 4)
-    pass_on(0, 1)
+    arrive(0, 1)
+    left_side(0, parts[1], 0, 2)
     pump(6)
+    left_side(0, parts[1], 2, 4)
     rest(0)
-    pump(7)
-    arrive(0, 1)
-    left_side(0, part[1], 0, 4)
-    acc[0] += right_side(part[1], 0, 4)
+    acc[0] += right_side(parts[1], 0, 4)
     for copy in c_far:
         came(copy)
     left_side(0, full, 4, 6)
@@ -337,24 +336,25 @@
             rows_of[n, m, 1] = jnp.concatenate([jnp.where(here, -imag, real), jnp.where(here, real, imag)], axis=0)
 
     arrive(1, 0)
-    left_side(1, part[0], 0, 8)
-    acc[1] = right_side(part[0], 0, 8)
+    left_side(1, parts[0], 0, 8)
+    acc[1] = right_side(parts[0], 0, 8)
     pass_on(1, 1)
     arrive(1, 1)
-    left_side(1, part[1], 0, 8)
-    total = acc[1] + right_side(part[1], 0, 8)
+    left_side(1, parts[1], 0, 8)
+    total = acc[1] + right_side(parts[1], 0, 8)
     own = edge_own[...].astype(F32)
     comb[0, 0, 0] = (total + weight_outer * own).astype(BF16)
     go(to_partner[0, 0])
     acc[1] = own + weight_edge * total
     came(to_beside[1])
-    go(over_across)
     came(to_across[0])
-    go(over_beside)
+    for r in range(2):
+        go(over_across[r])
+        go(over_beside[r])
     pass_on(2, 0)
     arrive(2, 0)
-    left_side(2, part[0], 0, 8)
-    acc[0] = right_side(part[0], 0, 8)
+    left_side(2, parts[0], 0, 8)
+    acc[0] = right_side(parts[0], 0, 8)
 
     def project(n, m, c):
         return jnp.dot(rows_of[n, m, c], comb[n, m, c], preferred_element_type=F32)
@@ -370,33 +370,37 @@
             middle[n, m] = project(n, m, 0)
     came(to_across[1])
     arrive(2, 1)
-    left_side(2, part[1], 0, 8)
-    acc[0] += right_side(part[1], 0, 8)
+    left_side(2, parts[1], 0, 8)
+    acc[0] += right_side(parts[1], 0, 8)
     comb[0, 0, 1] = (acc[0] + weight_outer * edge_other[...].astype(F32)).astype(BF16)
     go(to_partner[0, 1])
 
-    def finish(n, m):
-        e, s = (core, 1 - core)[n], (outer, edge)[m]
-        if n == 1:
-            came(to_partner[m, 1])
-        both = (middle[n, m] + project(n, m, 1)).astype(BF16)
-        real, imag = both[:rows], both[rows:]
-        sides = jnp.concatenate(
-            [jnp.concatenate([real, imag], axis=1), jnp.concatenate([imag, -real], axis=1)], axis=0
-        )
-        updated = by_rows(sides, jnp.concatenate([r_buf[e, s, 0], r_buf[e, s, 1]], axis=1))
-        out[e, s, 0] = updated[:rows]
-        out[e, s, 1] = updated[rows:]
-
-    finish(0, 0)
-    came(over_across)
-    came(over_beside)
-    around = acc[0] + near_other[...].astype(F32)
-    comb[0, 1, 1] = (edge_other[...].astype(F32) + weight_edge * around).astype(BF16)
-    go(to_partner[1, 1])
-    finish(1, 0)
-    finish(0, 1)
-    finish(1, 1)
+    def finish(n):
+        e = (core, 1 - core)[n]
+        both = [(middle[n, m] + project(n, m, 1)).astype(BF16) for m in range(2)]
+        for m, s in enumerate((outer, edge)):
+            real, imag = both[m][:rows], both[m][rows:]
+            sides = jnp.concatenate(
+                [jnp.concatenate([real, imag], axis=1), jnp.concatenate([imag, -real], axis=1)], axis=0
+            )
+            updated = by_rows(sides, jnp.concatenate([r_buf[e, s, 0], r_buf[e, s, 1]], axis=1))
+            out[e, s, 0] = updated[:rows]
+            out[e, s, 1] = updated[rows:]
+
+    def gather(r):
+        came(over_across[r])
+        came(over_beside[r])
+        rows = halves[r]
+        around = acc[0, rows] + near_other[rows].astype(F32)
+        comb[0, 1, 1, rows] = (edge_other[rows].astype(F32) + weight_edge * around).astype(BF16)
+        go(last_to_partner[r])
+
+    gather(0)
+    gather(1)
+    finish(0)
+    for copy in [to_partner[0, 1]] + last_to_partner:
+        came(copy)
+    finish(1)
 
     for n, (total, condition) in enumerate(groups):
         done = pltpu.make_async_remote_copy(
@@ -408,12 +412,11 @@
 
 def fast(lesser, retarded, coupling, occupations, offsets, intersection):
     nf, size, _ = coupling.shape
-    chunks = 2
     rows = size // 4
-    arrivals = 3 + 1 + BLOCKS + 1 + (BLOCKS - 1) + 4 + 3 * PIECES * chunks + 6 + 4
+    arrivals = 3 + 1 + 2 * len(RELAYS) + 2 + 4 + 6 * PIECES + 8 + 5
     anywhere = pl.BlockSpec(memory_space=pl.ANY)
     return pl.pallas_call(
-        functools.partial(kernel, chunks, lax.axis_size("energy")),
+        functools.partial(kernel, lax.axis_size("energy")),
         out_shape=pltpu.VMEM((2, 2, 2, rows, size), F32),
         in_specs=[anywhere] * 3 + [pl.BlockSpec(memory_space=pltpu.SMEM)] * 3,
         out_specs=pl.BlockSpec(memory_space=pltpu.VMEM),

time: 48 us -> 47.4 us (0.987)
  Pallas kernels: 46.5 us -> 45.9 us
    pallas_call x1, Pallas kernels: 46.5 us -> 45.9 us  [fast(): pl.pallas_call(functools.partial(kernel, lax.axis_size('energy')), out_sh...]
where the time goes in v4:
time: 47.4 us; the launch traced here: 47.3 us
  Pallas kernels  45.9 us (97%)
  local copies, waits for them, and re-layouts  1.32 us (3%)
    pallas_call x1, Pallas kernels, fast(): pl.pallas_call(functools.partial(kernel, lax.axis_size('energy')), out_sh...  45.9 us
    unnamed x1, local copies, waits for them, and re-layouts  1.32 us

profile of v4, /device:TPU:0, one launch (start us, length us, event | category | flops | bytes accessed | tf_op | source)
XLA Modules:
  0.0 47.3 jit_solution(10375279575781504709)
XLA Ops:
  0.0 45.9 %shard_map.64 = f32[2,2,2,128,512]{4,3,2,1,0:T(8,128)S(1)} custom-call(bf16[2,2,2,512,512]{4,3,2,1,0:T(8,128)(2,1)} %lesser.1, bf16[2,2,2,512,512]{4,3,2,1,0:T(8,128)(2,1)} %retarded.1, bf16[2,512,512]{2,1,0:T(8,128)(2,1)} %coupling.1, f32[2]{0:T(128)} %numbers.1, s32[2]{0:T(128)} %shifts.1, f32[2]{0:T(128)} %beside_weight.1), custom_call_target="tpu_custom_call" | custom-call | tf_op jit(solution)/shard_map/pallas_call | solution.py:418
  45.9 1.3 %copy.8 = f32[2,2,2,128,512]{4,3,2,1,0:T(8,128)} copy(f32[2,2,2,128,512]{4,3,2,1,0:T(8,128)S(1)} %shard_map.64) | data formatting | bytes 4194304

commit v5 on v4

--- a/solution.py
+++ b/solution.py
@@ -9,9 +9,10 @@
 OFFMAX = 2
 UNROLL = 8
 PIECES = 3
-RELAYS = (96, 96, 96, 64, 64, 32)
+RELAYS = (96, 96, 64, 64, 64, 32)
+SLIVER = 64
 EARLY = 3
-GROUPS = 14
+GROUPS = 16
 MESH = pl.DeviceIdType.MESH
 F32 = jnp.float32
 BF16 = jnp.bfloat16
@@ -191,15 +192,35 @@
     for_direct = group(c_buf.at[4, kept])
     c_across = [go(remote(coupling.at[x, rows], c_buf.at[4, rows], across, for_across)) for rows in rows_at + [kept]]
     c_direct = go(remote(coupling.at[1 - x, kept], c_buf.at[6, kept], across, for_direct))
-    for_z = group(green.at[:, pl.ds(0, 2)], has_to)
+    sliver, most = pl.ds(size - SLIVER, SLIVER), pl.ds(0, size - SLIVER)
+    for_z = group(green.at[pl.ds(0, 2), pl.ds(0, 2)], has_to)
+    for_last = group(green.at[2, pl.ds(0, 2), most], has_to)
     for_passed = group(green.at[:, 0], has_from)
+    for_side = group(green.at[1, pl.ds(0, 2), sliver], has_from)
     near, far, passed = {}, {}, {}
     for_near = group(coupling)
-    for p, (s, c) in enumerate(pieces):
+
+    def from_along(p, key, rows, columns, kind):
+        s, c = pieces[p]
+        near[p, key] = go(remote(lesser.at[1 - core, s, c, rows, columns], green.at[p, near_slot, rows, columns], along, kind))
+        far[p, key] = go(remote(lesser.at[core, s, c, rows, columns], green.at[p, far_slot, rows, columns], along, kind))
+
+    def to_pass(p, key, rows, columns):
+        passed[p, key] = remote(green.at[p, near_slot, rows, columns], green.at[p, pass_to, rows, columns], partner, for_passed)
+
+    every = pl.ds(0, size)
+    for p in range(PIECES):
+        if p == 1:
+            from_along(1, 2, sliver, every, for_z)
+            to_pass(1, 2, sliver, every)
+        if p == 2:
+            near[2, 2] = remote(green.at[1, near_slot, sliver], green.at[2, near_slot, sliver], across, for_side)
+            far[2, 2] = remote(green.at[1, far_slot, sliver], green.at[2, far_slot, sliver], across, for_side)
+            to_pass(2, 2, sliver, every)
         for k, columns in enumerate(parts):
-            near[p, k] = go(remote(lesser.at[1 - core, s, c, :, columns], green.at[p, near_slot, :, columns], along, for_z))
-            far[p, k] = go(remote(lesser.at[core, s, c, :, columns], green.at[p, far_slot, :, columns], along, for_z))
-            passed[p, k] = remote(green.at[p, near_slot, :, columns], green.at[p, pass_to, :, columns], partner, for_passed)
+            rows = every if p == 0 else most
+            from_along(p, k, rows, columns, for_last if p == 2 else for_z)
+            to_pass(p, k, rows, columns)
         if p == 0:
             c_near = go(remote(coupling, c_buf.at[pl.ds(nf, nf)], partner, for_near))
     for load in load_own[1:] + [load_r]:
@@ -261,11 +282,11 @@
 
         lax.fori_loop(start, stop, product, 0, unroll=min(UNROLL, stop - start))
 
-    def right_side(columns, start, stop):
-        def beside(ref):
-            return jnp.concatenate([ref[f, :, columns] for f in range(start, stop)], axis=1)
-
-        return by_rows(beside(left_buf), beside(c_buf))
+    def right_side(columns, start, stop, rows=slice(None)):
+        def beside(ref, rows):
+            return jnp.concatenate([ref[f, rows, columns] for f in range(start, stop)], axis=1)
+
+        return by_rows(beside(left_buf, rows), beside(c_buf, slice(None)))
 
     full = slice(0, size)
     halves = [pl.ds(h * half, half) for h in range(2)]
@@ -276,7 +297,8 @@
     over_across = [remote(near_own.at[rows, halves[1]], near_other.at[rows, halves[1]], across, for_over) for rows in halves]
     over_beside = [remote(edge_other.at[rows, halves[0]], near_other.at[rows, halves[0]], opposite, for_under) for rows in halves]
     for_comb = group(comb.at[0])
-    to_partner = {(m, c): remote(comb.at[0, m, c], comb.at[1, m, c], partner, for_comb) for m, c in ((0, 0), (1, 0), (0, 1))}
+    to_partner = [remote(comb.at[0, m, 0], comb.at[1, m, 0], partner, for_comb) for m in range(2)]
+    late_to_partner = [remote(comb.at[0, 0, 1, rows], comb.at[1, 0, 1, rows], partner, for_comb) for rows in halves]
     last_to_partner = [remote(comb.at[0, 1, 1, rows], comb.at[1, 1, 1, rows], partner, for_comb) for rows in halves]
     weight_outer, weight_edge = beside_weight[outer], beside_weight[edge]
 
@@ -307,16 +329,22 @@
     left_side(0, parts[1], 2, 4)
     rest(0)
     acc[0] += right_side(parts[1], 0, 4)
+    pass_on(1, 2)
+    pl.when(has_from)(far[1, 2][0].wait_recv)
+    go(near[2, 2])
+    go(far[2, 2])
     for copy in c_far:
         came(copy)
     left_side(0, full, 4, 6)
     rest(1)
     acc[0] += right_side(full, 4, 6)
     pass_on(1, 0)
+    left_side(0, full, 6, 7)
+    acc[0] += right_side(full, 6, 7)
     for copy in c_rest:
         came(copy)
-    left_side(0, full, 6, 8)
-    edge_own[...] = (acc[0] + right_side(full, 6, 8)).astype(BF16)
+    left_side(0, full, 7, 8)
+    edge_own[...] = (acc[0] + right_side(full, 7, 8)).astype(BF16)
     go(to_across[0])
     go(to_beside[1])
     go(to_across[1])
@@ -335,6 +363,8 @@
             rows_of[n, m, 0] = jnp.concatenate([jnp.where(here, real, -imag), jnp.where(here, imag, real)], axis=0)
             rows_of[n, m, 1] = jnp.concatenate([jnp.where(here, -imag, real), jnp.where(here, real, imag)], axis=0)
 
+    pass_on(2, 2)
+    pl.when(has_to)(passed[1, 2][0].wait_recv)
     arrive(1, 0)
     left_side(1, parts[0], 0, 8)
     acc[1] = right_side(parts[0], 0, 8)
@@ -344,7 +374,7 @@
     total = acc[1] + right_side(parts[1], 0, 8)
     own = edge_own[...].astype(F32)
     comb[0, 0, 0] = (total + weight_outer * own).astype(BF16)
-    go(to_partner[0, 0])
+    go(to_partner[0])
     acc[1] = own + weight_edge * total
     came(to_beside[1])
     came(to_across[0])
@@ -352,6 +382,7 @@
         go(over_across[r])
         go(over_beside[r])
     pass_on(2, 0)
+    arrive(2, 2)
     arrive(2, 0)
     left_side(2, parts[0], 0, 8)
     acc[0] = right_side(parts[0], 0, 8)
@@ -361,25 +392,27 @@
 
     came(to_beside[0])
     comb[0, 1, 0] = (acc[1] + weight_edge * near_own[...].astype(F32)).astype(BF16)
-    go(to_partner[1, 0])
+    go(to_partner[1])
     pass_on(2, 1)
     for n in range(2):
         for m in range(2):
             if n == 1:
-                came(to_partner[m, 0])
+                came(to_partner[m])
             middle[n, m] = project(n, m, 0)
     came(to_across[1])
     arrive(2, 1)
     left_side(2, parts[1], 0, 8)
-    acc[0] += right_side(parts[1], 0, 8)
-    comb[0, 0, 1] = (acc[0] + weight_outer * edge_other[...].astype(F32)).astype(BF16)
-    go(to_partner[0, 1])
-
-    def finish(n):
-        e = (core, 1 - core)[n]
-        both = [(middle[n, m] + project(n, m, 1)).astype(BF16) for m in range(2)]
-        for m, s in enumerate((outer, edge)):
-            real, imag = both[m][:rows], both[m][rows:]
+    for h, rows in enumerate(halves):
+        acc[0, rows] += right_side(parts[1], 0, 8, rows)
+        comb[0, 0, 1, rows] = (acc[0, rows] + weight_outer * edge_other[rows].astype(F32)).astype(BF16)
+        go(late_to_partner[h])
+    rows = size // 4
+
+    def finish(*blocks):
+        both = [(middle[n, m] + project(n, m, 1)).astype(BF16) for n, m in blocks]
+        for (n, m), sums in zip(blocks, both):
+            e, s = (core, 1 - core)[n], (outer, edge)[m]
+            real, imag = sums[:rows], sums[rows:]
             sides = jnp.concatenate(
                 [jnp.concatenate([real, imag], axis=1), jnp.concatenate([imag, -real], axis=1)], axis=0
             )
@@ -397,10 +430,13 @@
 
     gather(0)
     gather(1)
-    finish(0)
-    for copy in [to_partner[0, 1]] + last_to_partner:
+    finish((0, 0), (0, 1))
+    for copy in late_to_partner:
         came(copy)
-    finish(1)
+    finish((1, 0))
+    for copy in last_to_partner:
+        came(copy)
+    finish((1, 1))
 
     for n, (total, condition) in enumerate(groups):
         done = pltpu.make_async_remote_copy(
@@ -413,7 +449,7 @@
 def fast(lesser, retarded, coupling, occupations, offsets, intersection):
     nf, size, _ = coupling.shape
     rows = size // 4
-    arrivals = 3 + 1 + 2 * len(RELAYS) + 2 + 4 + 6 * PIECES + 8 + 5
+    arrivals = 3 + 1 + 2 * len(RELAYS) + 2 + 4 + 6 * PIECES + 6 + 8 + 6
     anywhere = pl.BlockSpec(memory_space=pl.ANY)
     return pl.pallas_call(
         functools.partial(kernel, lax.axis_size("energy")),

time: 47.4 us -> 46.2 us (0.975)
  Pallas kernels: 45.9 us -> 44.7 us
    pallas_call x1, Pallas kernels: 45.9 us -> 44.7 us  [fast(): pl.pallas_call(functools.partial(kernel, lax.axis_size('energy')), out_sh...]
where the time goes in v5:
time: 46.2 us; the launch traced here: 46 us
  Pallas kernels  44.7 us (97%)
  local copies, waits for them, and re-layouts  1.32 us (3%)
    pallas_call x1, Pallas kernels, fast(): pl.pallas_call(functools.partial(kernel, lax.axis_size('energy')), out_sh...  44.7 us
    unnamed x1, local copies, waits for them, and re-layouts  1.32 us

profile of v5, /device:TPU:0, one launch (start us, length us, event | category | flops | bytes accessed | tf_op | source)
XLA Modules:
  0.0 46.0 jit_solution(15063223843724872759)
XLA Ops:
  0.0 44.7 %shard_map.64 = f32[2,2,2,128,512]{4,3,2,1,0:T(8,128)S(1)} custom-call(bf16[2,2,2,512,512]{4,3,2,1,0:T(8,128)(2,1)} %lesser.1, bf16[2,2,2,512,512]{4,3,2,1,0:T(8,128)(2,1)} %retarded.1, bf16[2,512,512]{2,1,0:T(8,128)(2,1)} %coupling.1, f32[2]{0:T(128)} %numbers.1, s32[2]{0:T(128)} %shifts.1, f32[2]{0:T(128)} %beside_weight.1), custom_call_target="tpu_custom_call" | custom-call | tf_op jit(solution)/shard_map/pallas_call | solution.py:454
  44.7 1.3 %copy.8 = f32[2,2,2,128,512]{4,3,2,1,0:T(8,128)} copy(f32[2,2,2,128,512]{4,3,2,1,0:T(8,128)S(1)} %shard_map.64) | data formatting | bytes 4194304

commit v6 on v5

--- a/solution.py
+++ b/solution.py
@@ -9,7 +9,7 @@
 OFFMAX = 2
 UNROLL = 8
 PIECES = 3
-RELAYS = (96, 96, 64, 64, 64, 32)
+RELAYS = (96, 96, 64, 64, 64, 48)
 SLIVER = 64
 EARLY = 3
 GROUPS = 16
@@ -294,12 +294,13 @@
     to_across = [remote(edge_own.at[:, columns], edge_other.at[:, columns], across, for_edge) for columns in halves]
     to_beside = [remote(edge_own.at[:, columns], near_own.at[:, columns], opposite, for_beside) for columns in halves]
     for_over, for_under = group(near_own.at[:, halves[1]]), group(near_own.at[:, halves[1]])
-    over_across = [remote(near_own.at[rows, halves[1]], near_other.at[rows, halves[1]], across, for_over) for rows in halves]
-    over_beside = [remote(edge_other.at[rows, halves[0]], near_other.at[rows, halves[0]], opposite, for_under) for rows in halves]
+    uneven = [pl.ds(0, size - size // 4), pl.ds(size - size // 4, size // 4)]
+    over_across = [remote(near_own.at[rows, halves[1]], near_other.at[rows, halves[1]], across, for_over) for rows in uneven]
+    over_beside = [remote(edge_other.at[rows, halves[0]], near_other.at[rows, halves[0]], opposite, for_under) for rows in uneven]
     for_comb = group(comb.at[0])
     to_partner = [remote(comb.at[0, m, 0], comb.at[1, m, 0], partner, for_comb) for m in range(2)]
     late_to_partner = [remote(comb.at[0, 0, 1, rows], comb.at[1, 0, 1, rows], partner, for_comb) for rows in halves]
-    last_to_partner = [remote(comb.at[0, 1, 1, rows], comb.at[1, 1, 1, rows], partner, for_comb) for rows in halves]
+    last_to_partner = [remote(comb.at[0, 1, 1, rows], comb.at[1, 1, 1, rows], partner, for_comb) for rows in uneven]
     weight_outer, weight_edge = beside_weight[outer], beside_weight[edge]
 
     fill(0)
@@ -423,17 +424,17 @@
     def gather(r):
         came(over_across[r])
         came(over_beside[r])
-        rows = halves[r]
+        rows = uneven[r]
         around = acc[0, rows] + near_other[rows].astype(F32)
         comb[0, 1, 1, rows] = (edge_other[rows].astype(F32) + weight_edge * around).astype(BF16)
         go(last_to_partner[r])
 
     gather(0)
+    finish((0, 0))
     gather(1)
-    finish((0, 0), (0, 1))
     for copy in late_to_partner:
         came(copy)
-    finish((1, 0))
+    finish((0, 1), (1, 0))
     for copy in last_to_partner:
         came(copy)
     finish((1, 1))

time: 46.2 us -> 45.8 us (level)
  no operation moved by 1% of the time
where the time goes in v6:
time: 45.8 us; the launch traced here: 45.7 us
  Pallas kernels  44.3 us (97%)
  local copies, waits for them, and re-layouts  1.32 us (3%)
    pallas_call x1, Pallas kernels, fast(): pl.pallas_call(functools.partial(kernel, lax.axis_size('energy')), out_sh...  44.3 us
    unnamed x1, local copies, waits for them, and re-layouts  1.32 us

profile of v6, /device:TPU:0, one launch (start us, length us, event | category | flops | bytes accessed | tf_op | source)
XLA Modules:
  0.0 45.7 jit_solution(11134252440341933888)
XLA Ops:
  0.0 44.3 %shard_map.64 = f32[2,2,2,128,512]{4,3,2,1,0:T(8,128)S(1)} custom-call(bf16[2,2,2,512,512]{4,3,2,1,0:T(8,128)(2,1)} %lesser.1, bf16[2,2,2,512,512]{4,3,2,1,0:T(8,128)(2,1)} %retarded.1, bf16[2,512,512]{2,1,0:T(8,128)(2,1)} %coupling.1, f32[2]{0:T(128)} %numbers.1, s32[2]{0:T(128)} %shifts.1, f32[2]{0:T(128)} %beside_weight.1), custom_call_target="tpu_custom_call" | custom-call | tf_op jit(solution)/shard_map/pallas_call | solution.py:455
  44.4 1.3 %copy.8 = f32[2,2,2,128,512]{4,3,2,1,0:T(8,128)} copy(f32[2,2,2,128,512]{4,3,2,1,0:T(8,128)S(1)} %shard_map.64) | data formatting | bytes 4194304

commit v7 on v6

--- a/solution.py
+++ b/solution.py
@@ -12,7 +12,7 @@
 RELAYS = (96, 96, 64, 64, 64, 48)
 SLIVER = 64
 EARLY = 3
-GROUPS = 16
+GROUPS = 8
 MESH = pl.DeviceIdType.MESH
 F32 = jnp.float32
 BF16 = jnp.bfloat16
@@ -188,8 +188,8 @@
     for_w = group(w_tile.at[pl.ds(0, 3)])
     w_in = [go(remote(w_tile.at[0], w_tile.at[d + 1], peer, for_w)) for d, peer in enumerate((partner, across))]
     w_on = remote(w_tile.at[2], w_tile.at[3], partner, for_w)
-    for_across = group(c_buf.at[4])
-    for_direct = group(c_buf.at[4, kept])
+    for_blocks = for_across = for_direct = group(green.at[0])
+    for_sums = group(c_buf)
     c_across = [go(remote(coupling.at[x, rows], c_buf.at[4, rows], across, for_across)) for rows in rows_at + [kept]]
     c_direct = go(remote(coupling.at[1 - x, kept], c_buf.at[6, kept], across, for_direct))
     sliver, most = pl.ds(size - SLIVER, SLIVER), pl.ds(0, size - SLIVER)
@@ -198,7 +198,7 @@
     for_passed = group(green.at[:, 0], has_from)
     for_side = group(green.at[1, pl.ds(0, 2), sliver], has_from)
     near, far, passed = {}, {}, {}
-    for_near = group(coupling)
+    for_near = for_sums
 
     def from_along(p, key, rows, columns, kind):
         s, c = pieces[p]
@@ -226,10 +226,11 @@
     for load in load_own[1:] + [load_r]:
         load.start()
 
-    for_relay, for_far, for_rest = group(c_buf.at[4, pl.ds(0, starts[-1])]), group(c_buf.at[4]), group(c_buf.at[6])
+    for_relay = for_far = for_rest = for_blocks
     relayed = [remote(c_buf.at[4, rows], c_buf.at[6, rows], opposite, for_relay) for rows in rows_at]
     c_far = [remote(c_buf.at[4, rows], c_buf.at[5, rows], partner, for_far) for rows in staged]
-    c_rest = [remote(c_buf.at[6, rows], c_buf.at[7, rows], partner, for_rest) for rows in staged]
+    stages = [staged[0], pl.ds(starts[EARLY], starts[-1] - starts[EARLY]), kept]
+    c_rest = [remote(c_buf.at[6, rows], c_buf.at[7, rows], partner, for_rest) for rows in stages]
 
     def pump(b):
         came(c_across[b])
@@ -241,7 +242,7 @@
             go(c_far[1])
 
     def rest(h):
-        for copy in (relayed[EARLY:] + [c_direct]) if h else relayed[:EARLY]:
+        for copy in (relayed[:EARLY], relayed[EARLY:], [c_direct])[h]:
             came(copy)
         go(c_rest[h])
 
@@ -290,14 +291,14 @@
 
     full = slice(0, size)
     halves = [pl.ds(h * half, half) for h in range(2)]
-    for_edge, for_beside = group(edge_own), group(edge_own)
+    for_edge = for_beside = for_sums
     to_across = [remote(edge_own.at[:, columns], edge_other.at[:, columns], across, for_edge) for columns in halves]
     to_beside = [remote(edge_own.at[:, columns], near_own.at[:, columns], opposite, for_beside) for columns in halves]
-    for_over, for_under = group(near_own.at[:, halves[1]]), group(near_own.at[:, halves[1]])
+    for_over = for_under = group(edge_own)
     uneven = [pl.ds(0, size - size // 4), pl.ds(size - size // 4, size // 4)]
     over_across = [remote(near_own.at[rows, halves[1]], near_other.at[rows, halves[1]], across, for_over) for rows in uneven]
     over_beside = [remote(edge_other.at[rows, halves[0]], near_other.at[rows, halves[0]], opposite, for_under) for rows in uneven]
-    for_comb = group(comb.at[0])
+    for_comb = for_sums
     to_partner = [remote(comb.at[0, m, 0], comb.at[1, m, 0], partner, for_comb) for m in range(2)]
     late_to_partner = [remote(comb.at[0, 0, 1, rows], comb.at[1, 0, 1, rows], partner, for_comb) for rows in halves]
     last_to_partner = [remote(comb.at[0, 1, 1, rows], comb.at[1, 1, 1, rows], partner, for_comb) for rows in uneven]
@@ -338,6 +339,7 @@
         came(copy)
     left_side(0, full, 4, 6)
     rest(1)
+    rest(2)
     acc[0] += right_side(full, 4, 6)
     pass_on(1, 0)
     left_side(0, full, 6, 7)
@@ -450,7 +452,7 @@
 def fast(lesser, retarded, coupling, occupations, offsets, intersection):
     nf, size, _ = coupling.shape
     rows = size // 4
-    arrivals = 3 + 1 + 2 * len(RELAYS) + 2 + 4 + 6 * PIECES + 6 + 8 + 6
+    arrivals = 3 + 1 + 2 * len(RELAYS) + 2 + 5 + 6 * PIECES + 6 + 8 + 6
     anywhere = pl.BlockSpec(memory_space=pl.ANY)
     return pl.pallas_call(
         functools.partial(kernel, lax.axis_size("energy")),

time: 45.8 us -> 45.8 us (level)
  no operation moved by 1% of the time
where the time goes in v7:
time: 45.8 us; the launch traced here: 45.6 us
  Pallas kernels  44.3 us (97%)
  local copies, waits for them, and re-layouts  1.32 us (3%)
    pallas_call x1, Pallas kernels, fast(): pl.pallas_call(functools.partial(kernel, lax.axis_size('energy')), out_sh...  44.3 us
    unnamed x1, local copies, waits for them, and re-layouts  1.32 us

profile of v7, /device:TPU:0, one launch (start us, length us, event | category | flops | bytes accessed | tf_op | source)
XLA Modules:
  0.0 45.6 jit_solution(14378735163751824628)
XLA Ops:
  0.0 44.3 %shard_map.64 = f32[2,2,2,128,512]{4,3,2,1,0:T(8,128)S(1)} custom-call(bf16[2,2,2,512,512]{4,3,2,1,0:T(8,128)(2,1)} %lesser.1, bf16[2,2,2,512,512]{4,3,2,1,0:T(8,128)(2,1)} %retarded.1, bf16[2,512,512]{2,1,0:T(8,128)(2,1)} %coupling.1, f32[2]{0:T(128)} %numbers.1, s32[2]{0:T(128)} %shifts.1, f32[2]{0:T(128)} %beside_weight.1), custom_call_target="tpu_custom_call" | custom-call | tf_op jit(solution)/shard_map/pallas_call | solution.py:457
  44.3 1.3 %copy.8 = f32[2,2,2,128,512]{4,3,2,1,0:T(8,128)} copy(f32[2,2,2,128,512]{4,3,2,1,0:T(8,128)S(1)} %shard_map.64) | data formatting | bytes 4194304
